TPU v7x, 256 devices: a whole 4x4x8 slice. The times are simulated.
256 devices in a mesh: shot: 8 (over y, core), gx: 8 (over z), gy: 4 (over x).
Axes of the slice: x: 4, y: 4, z: 8, core: 2. Of those that a mesh axis runs over, the one named last changes fastest.
Arguments:
- vel_coef: float32 [256, 128, 128], P('gx', 'gy'), may hold values from 0.03 to 0.2
- src_prev: float32 [8, 256, 128, 128], P('shot', 'gx', 'gy'), may hold values from -6 to 6
- src_cur: float32 [8, 256, 128, 128], P('shot', 'gx', 'gy'), may hold values from -6 to 6
- rcv_prev: float32 [8, 256, 128, 128], P('shot', 'gx', 'gy'), may hold values from -6 to 6
- rcv_cur: float32 [8, 256, 128, 128], P('shot', 'gx', 'gy'), may hold values from -6 to 6
- src_pos: int32 [8], P('shot'), may hold values from 0 to 4194303
- src_amp: float32 [8, 3], P('shot'), may hold values from -24 to 24
- rcv_pos: int32 [8, 512], P('shot'), may hold values from 0 to 4194303
- rcv_data: float32 [8, 3, 512], P('shot'), may hold values from -6 to 6
- aperture: int32 [8, 16], P('shot'), may hold values from 0 to 31, as said below
- owner: int32 [32, 32], replicated, may hold values from 0 to 31, as said below
Outputs:
- src_next: float32 [8, 256, 128, 128], P('shot', 'gx', 'gy')
- rcv_next: float32 [8, 256, 128, 128], P('shot', 'gx', 'gy')
- gathers: float32 [32, 16, 32, 1, 32, 128], P(('gx', 'gy'), 'shot')
Inputs may be any that keep to these rules, and one draw needn't show every extreme that they name: `aperture`: each row lists 16 different tiles. `owner`: each row and each column holds every tile number once.
All inputs are finite; a program needn't handle non-finite values.
Results may differ from a plain program's by a relative error of at most 0.0003.
Values sent between devices are 32-bit elements; how exact they have to be, the bound alone decides.
A program may use at most 64 MiB of HBM per device.

v0:
```python
import jax
import jax.numpy as jnp
from jax import lax
from jax.sharding import PartitionSpec as P

OFFS = 16
STEPS = 3
HALF = 8


LAP_CENTER = -2.5
LAP_NEAR = 4.0 / 3.0
LAP_FAR = -1.0 / 12.0


def padded(cells, sides, width):
    for axis, dim in sides:
        count = lax.axis_size(axis)
        ends = count - 1
        head = lax.slice_in_dim(cells, 0, width, axis=dim)
        tail = lax.slice_in_dim(cells, cells.shape[dim] - width, cells.shape[dim], axis=dim)
        cells = jnp.concatenate(
            [
                lax.ppermute(tail, axis, [(i, (i + 1) % count) for i in range(ends)]),
                cells,
                lax.ppermute(head, axis, [((i + 1) % count, i) for i in range(ends)]),
            ],
            axis=dim,
        )
    return cells


def laplacian(widened):
    centre = widened[..., 2:-2, 2:-2, :]
    summed = 3.0 * LAP_CENTER * centre
    summed = summed + LAP_NEAR * (widened[..., 3:-1, 2:-2, :] + widened[..., 1:-3, 2:-2, :])
    summed = summed + LAP_FAR * (widened[..., 4:, 2:-2, :] + widened[..., :-4, 2:-2, :])
    summed = summed + LAP_NEAR * (widened[..., 2:-2, 3:-1, :] + widened[..., 2:-2, 1:-3, :])
    summed = summed + LAP_FAR * (widened[..., 2:-2, 4:, :] + widened[..., 2:-2, :-4, :])
    depth_pad = jnp.pad(centre, [(0, 0)] * (centre.ndim - 1) + [(2, 2)])
    summed = summed + LAP_NEAR * (depth_pad[..., 3:-1] + depth_pad[..., 1:-3])
    summed = summed + LAP_FAR * (depth_pad[..., 4:] + depth_pad[..., :-4])
    return summed


def inject(field_in, positions, values, anchor_x, anchor_y, grid_y, depth_cells):
    ext_x, ext_y = (field_in.shape[0], field_in.shape[1])
    plane_cells = grid_y * depth_cells
    local_x = positions // plane_cells - anchor_x
    local_y = positions // depth_cells % grid_y - anchor_y
    local_z = positions % depth_cells
    inside = (local_x >= 0) & (local_x < ext_x) & (local_y >= 0) & (local_y < ext_y)
    flat_index = jnp.where(
        inside, (local_x * ext_y + local_y) * depth_cells + local_z, ext_x * ext_y * depth_cells
    )
    flat_field = field_in.reshape(-1).at[flat_index].add(values, mode="drop")
    return flat_field.reshape(field_in.shape)


def body(
    vel_coef,
    src_prev,
    src_cur,
    rcv_prev,
    rcv_cur,
    src_pos,
    src_amp,
    rcv_pos,
    rcv_data,
    aperture,
    owner,
):
    width_x, width_y, depth_cells = vel_coef.shape
    tile_count = lax.axis_size("gx") * lax.axis_size("gy")
    grid_y = width_y * lax.axis_size("gy")
    start_x = lax.axis_index("gx") * width_x
    start_y = lax.axis_index("gy") * width_y
    tile_id = lax.axis_index(("gx", "gy"))
    snapshots = []
    previous = jnp.concatenate([src_prev, rcv_prev], 0)
    current = jnp.concatenate([src_cur, rcv_cur], 0)
    for step_index in range(STEPS):
        widened = padded(current, (("gx", 1), ("gy", 2)), 2)
        updated = 2.0 * current - previous + vel_coef * laplacian(widened)
        source_field = inject(
            updated[0], src_pos, src_amp[:, step_index], start_x, start_y, grid_y, depth_cells
        )
        receiver_field = inject(
            updated[1], rcv_pos[0], rcv_data[0, step_index], start_x, start_y, grid_y, depth_cells
        )
        updated = jnp.stack([source_field, receiver_field])
        previous, current = (current, updated)
        snapshots.append(padded(current, (("gx", 1),), HALF))
    in_aperture = jnp.any(aperture[0] == tile_id)

    def correlate():
        offset_rows = []
        for offset_index in range(OFFS):
            lead_start = 2 * HALF - offset_index
            summed = None
            for snapshot in snapshots:
                product_term = (
                    snapshot[0, lead_start : lead_start + width_x]
                    * snapshot[1, offset_index : offset_index + width_x]
                )
                summed = product_term if summed is None else summed + product_term
            offset_rows.append(summed)
        return jnp.stack(offset_rows)

    def nothing_here():
        return jnp.zeros((OFFS, width_x, width_y, depth_cells), jnp.float32)

    partial_image = lax.cond(in_aperture, correlate, nothing_here)
    strip_rows = width_x // tile_count
    strips = partial_image.reshape(OFFS, tile_count, strip_rows, width_y, depth_cells)
    owner_row = lax.dynamic_index_in_dim(owner, tile_id, 0, keepdims=False)
    tile_numbers = jnp.arange(tile_count, dtype=jnp.int32)
    matches = owner_row[:, None] == tile_numbers[None, :]
    strip_for = jnp.sum(jnp.where(matches, tile_numbers[:, None], 0), axis=0)
    outgoing = jnp.take(strips, strip_for, axis=1)
    reduced = lax.psum_scatter(outgoing, "shot", scatter_dimension=0, tiled=True)
    arrived = lax.all_to_all(reduced, ("gx", "gy"), split_axis=1, concat_axis=1, tiled=True)
    return (current[0:1], current[1:2], arrived[None])


def solution(mesh):
    return jax.shard_map(
        body,
        mesh=mesh,
        in_specs=(
            P("gx", "gy", None),
            P("shot", "gx", "gy", None),
            P("shot", "gx", "gy", None),
            P("shot", "gx", "gy", None),
            P("shot", "gx", "gy", None),
            P("shot"),
            P("shot", None),
            P("shot", None),
            P("shot", None, None),
            P("shot", None),
            P(),
        ),
        out_specs=(
            P("shot", "gx", "gy", None),
            P("shot", "gx", "gy", None),
            P(("gx", "gy"), "shot", None, None, None, None),
        ),
        check_vma=False,
    )
```

profile of v0, /device:TPU:1, one launch (start us, length us, event | category | flops | bytes accessed | tf_op | source)
XLA Modules:
  0.0 297.0 jit_solution(6599415307512286985)
XLA Ops:
  10.7 5.0 %collective-permute-start.1 = (f32[2,2,32,128]{3,2,1,0:T(8,128)S(1)}, f32[2,2,32,128]{3,2,1,0:T(8,128)S(1)}, u32[]{:S(2)}, u32[]{:S(2)}) collective-permute-start(f32[2,2,32,128]{3,2,1,0:T(8,128)S(1)} %get-tuple-element.113), channel_id=1, source_target_pairs={{0,4},{4,8},{8,12},{12,16},{16,20},{20,24},{24,28},{1,5},{5,9},{9,... | collective-permute-start | bytes 196616 | tf_op jit(solution)/shard_map/ppermute | solution.py:24
  20.5 4.0 %collective-permute-start.3 = (f32[2,36,2,128]{3,2,1,0:T(2,128)S(1)}, f32[2,36,2,128]{3,2,1,0:T(2,128)S(1)}, u32[]{:S(2)}, u32[]{:S(2)}) collective-permute-start(f32[2,36,2,128]{3,2,1,0:T(2,128)S(1)} %get-tuple-element.91), channel_id=1, source_target_pairs={{0,1},{1,2},{2,3},{4,5},{5,6},{6,7},{8,9},{9,10},{10,11},{12,13},{... | collective-permute-start | bytes 221192 | tf_op jit(solution)/shard_map/ppermute | solution.py:24
  26.2 1.8 fusion.10
  28.0 2.1 fusion.63
  30.2 3.5 %scatter_fusion = f32[131072]{0:T(1024)S(1)} fusion(f32[131072]{0:T(1024)S(1)} %bitcast.67, s32[512]{0:T(512)S(1)} %bitcast.111, f32[512]{0:T(512)S(1)} %bitcast.116), kind=kCustom, calls=%fused_computation.1 | custom fusion | flops 512 | bytes 8192 | tf_op jit(solution)/shard_map/scatter-add | solution.py:56
  35.1 4.2 %collective-permute-start.5 = (f32[2,2,32,128]{3,2,1,0:T(8,128)S(1)}, f32[2,2,32,128]{3,2,1,0:T(8,128)S(1)}, u32[]{:S(2)}, u32[]{:S(2)}) collective-permute-start(f32[2,2,32,128]{3,2,1,0:T(8,128)S(1)} %get-tuple-element.108), channel_id=1, source_target_pairs={{0,4},{4,8},{8,12},{12,16},{16,20},{20,24},{24,28},{1,5},{5,9},{9,... | collective-permute-start | bytes 196616 | tf_op jit(solution)/shard_map/ppermute | solution.py:24
  40.2 3.5 %collective-permute-start.12 = (f32[2,8,32,128]{3,2,1,0:T(8,128)}, f32[2,8,32,128]{3,2,1,0:T(8,128)S(1)}, u32[]{:S(2)}, u32[]{:S(2)}) collective-permute-start(f32[2,8,32,128]{3,2,1,0:T(8,128)} %get-tuple-element.96), channel_id=1, source_target_pairs={{0,4},{4,8},{8,12},{12,16},{16,20},{20,24},{24,28},{1,5},{5,9},{9,... | collective-permute-start | bytes 786440 | tf_op jit(solution)/shard_map/ppermute | solution.py:24
  46.4 4.3 %collective-permute-start.7 = (f32[2,36,2,128]{3,2,1,0:T(2,128)S(1)}, f32[2,36,2,128]{3,2,1,0:T(2,128)S(1)}, u32[]{:S(2)}, u32[]{:S(2)}) collective-permute-start(f32[2,36,2,128]{3,2,1,0:T(2,128)S(1)} %get-tuple-element.87), channel_id=1, source_target_pairs={{0,1},{1,2},{2,3},{4,5},{5,6},{6,7},{8,9},{9,10},{10,11},{12,13},{... | collective-permute-start | bytes 221192 | tf_op jit(solution)/shard_map/ppermute | solution.py:24
  53.8 2.1 fusion.64
  55.9 3.5 %scatter_fusion.1 = f32[131072]{0:T(1024)S(1)} fusion(f32[131072]{0:T(1024)S(1)} %bitcast.76, s32[512]{0:T(512)S(1)} %bitcast.112, f32[512]{0:T(512)S(1)} %bitcast.115), kind=kCustom, calls=%fused_computation.2 | custom fusion | flops 512 | bytes 8192 | tf_op jit(solution)/shard_map/scatter-add | solution.py:56
  60.9 6.0 %collective-permute-start.9 = (f32[2,2,32,128]{3,2,1,0:T(8,128)S(1)}, f32[2,2,32,128]{3,2,1,0:T(8,128)S(1)}, u32[]{:S(2)}, u32[]{:S(2)}) collective-permute-start(f32[2,2,32,128]{3,2,1,0:T(8,128)S(1)} %get-tuple-element.102), channel_id=1, source_target_pairs={{0,4},{4,8},{8,12},{12,16},{16,20},{20,24},{24,28},{1,5},{5,9},{9,... | collective-permute-start | bytes 196616 | tf_op jit(solution)/shard_map/ppermute | solution.py:24
  67.8 4.6 %collective-permute-start.14 = (f32[2,8,32,128]{3,2,1,0:T(8,128)}, f32[2,8,32,128]{3,2,1,0:T(8,128)S(1)}, u32[]{:S(2)}, u32[]{:S(2)}) collective-permute-start(f32[2,8,32,128]{3,2,1,0:T(8,128)} %get-tuple-element.94), channel_id=1, source_target_pairs={{0,4},{4,8},{8,12},{12,16},{16,20},{20,24},{24,28},{1,5},{5,9},{9,... | collective-permute-start | bytes 786440 | tf_op jit(solution)/shard_map/ppermute | solution.py:24
  73.7 4.6 %collective-permute-start.11 = (f32[2,36,2,128]{3,2,1,0:T(2,128)S(1)}, f32[2,36,2,128]{3,2,1,0:T(2,128)S(1)}, u32[]{:S(2)}, u32[]{:S(2)}) collective-permute-start(f32[2,36,2,128]{3,2,1,0:T(2,128)S(1)} %get-tuple-element.83), channel_id=1, source_target_pairs={{0,1},{1,2},{2,3},{4,5},{5,6},{6,7},{8,9},{9,10},{10,11},{12,13},{... | collective-permute-start | bytes 221192 | tf_op jit(solution)/shard_map/ppermute | solution.py:24
  80.2 1.4 fusion.29
  81.7 3.5 %scatter_fusion.2 = f32[131072]{0:T(1024)S(1)} fusion(f32[131072]{0:T(1024)S(1)} %bitcast.101, s32[512]{0:T(512)S(1)} %bitcast.113, f32[512]{0:T(512)S(1)} %bitcast.114), kind=kCustom, calls=%fused_computation.3 | custom fusion | flops 512 | bytes 8192 | tf_op jit(solution)/shard_map/scatter-add | solution.py:56
  85.3 2.1 fusion.65
  87.5 4.0 %collective-permute-start.16 = (f32[2,8,32,128]{3,2,1,0:T(8,128)S(1)}, f32[2,8,32,128]{3,2,1,0:T(8,128)S(1)}, u32[]{:S(2)}, u32[]{:S(2)}) collective-permute-start(f32[2,8,32,128]{3,2,1,0:T(8,128)S(1)} %get-tuple-element.92), channel_id=1, source_target_pairs={{0,4},{4,8},{8,12},{12,16},{16,20},{20,24},{24,28},{1,5},{5,9},{9,... | collective-permute-start | bytes 786440 | tf_op jit(solution)/shard_map/ppermute | solution.py:24
  91.5 1.4 collective-permute-start.17
  94.8 5.2 %collective-permute-done.17 = f32[2,8,32,128]{3,2,1,0:T(8,128)S(1)} collective-permute-done((f32[2,8,32,128]{3,2,1,0:T(8,128)S(1)}, f32[2,8,32,128]{3,2,1,0:T(8,128)S(1)}, u32[]{:S(2)}, u32[]{:S(2)}) %collective-permute-start.17) | collective-permute-done | bytes 262176 | tf_op jit(solution)/shard_map/ppermute | solution.py:26
  100.1 18.7 %conditional.1 = (f32[16,32,32,128]{3,2,1,0:T(8,128)}) conditional(s32[]{:T(128)} %convert_element_type.7, () %tuple.28, (f32[2,48,32,128]{3,2,1,0:T(8,128)S(1)}, f32[2,48,32,128]{3,2,1,0:T(8,128)S(1)}, f32[2,48,32,128]{3,2,1,0:T(8,128)S(1)}, f32[131072]{0:T(1024)S(1)}, f32[131072]{0:T(1024)S(1)}, /*index=5*/f32[131072]{0:T(1024)S(1)}, ...), branch_computations={%region_5.6_spmd, %region_6.7_spmd} | conditional | flops 10485759 | bytes 59768840 | solution.py:113
  118.8 7.7 %gather_fusion = f32[32,16,32,128]{3,2,1,0:T(8,128)} fusion(f32[16,32,32,128]{3,2,1,0:T(8,128)} %get-tuple-element.79, s32[1024]{0:T(1024)S(1)} %pad_clamp_fusion), kind=kCustom, calls=%fused_computation | custom fusion | bytes 16777344 | tf_op jit(solution)/shard_map/jit(_take)/gather | solution.py:120
  126.5 8.3 %bitcast_select_fusion = f32[16,32,1,32,128]{4,3,0,1,2:T(8,128)} fusion(f32[32,16,32,128]{3,2,1,0:T(8,128)} %gather_fusion, pred[32]{0:T(512)(128)(4,1)S(1)} %compare_and_fusion), kind=kLoop, calls=%fused_computation.21 | loop fusion | flops 2097152 | bytes 16777248 | tf_op jit(solution)/shard_map/jit(_take)/select_n | solution.py:120
  136.8 115.6 %all-reduce.6.cloned.1.call-done = f32[16,32,1,32,128]{4,3,0,1,2:T(8,128)} async-done(((f32[16,32,1,32,128]{4,3,0,1,2:T(8,128)}), f32[16,32,1,32,128]{4,3,0,1,2:T(8,128)}) %all-reduce.6.cloned.1.call-update) | async-done | bytes 8388624
  253.7 35.4 %all_to_all.5 = f32[2,32,1,32,128]{4,3,0,2,1:T(8,128)S(1)} all-to-all(f32[2,32,1,32,128]{4,3,0,2,1:T(8,128)S(1)} %dynamic-slice_bitcast_fusion), channel_id=1, replica_groups=mesh['shot'=8,'gx'=8,'gy'=4] {'gx','gy'}, dimensions={1} | all-to-all | bytes 2097152 | tf_op jit(solution)/shard_map/all_to_all | solution.py:122
  (121 shorter events, 45.5 us)
Async XLA Ops:
  7.2 245.1 %all-reduce.6.cloned.1.call-start = ((), (), s32[]{:S(2)}) async-start(), calls=%async_computation.1 | async-start | bytes 16777216
  9.4 9.7 %collective-permute-start = (f32[2,2,32,128]{3,2,1,0:T(8,128)S(1)}, f32[2,2,32,128]{3,2,1,0:T(8,128)S(1)}, u32[]{:S(2)}, u32[]{:S(2)}) collective-permute-start(f32[2,2,32,128]{3,2,1,0:T(8,128)S(1)} %get-tuple-element.112), channel_id=1, source_target_pairs={{4,0},{8,4},{12,8},{16,12},{20,16},{24,20},{28,24},{5,1},{9,5},{13... | collective-permute-start | bytes 196616 | tf_op jit(solution)/shard_map/ppermute | solution.py:26
  10.7 8.4 %collective-permute-start.1 = (f32[2,2,32,128]{3,2,1,0:T(8,128)S(1)}, f32[2,2,32,128]{3,2,1,0:T(8,128)S(1)}, u32[]{:S(2)}, u32[]{:S(2)}) collective-permute-start(f32[2,2,32,128]{3,2,1,0:T(8,128)S(1)} %get-tuple-element.113), channel_id=1, source_target_pairs={{0,4},{4,8},{8,12},{12,16},{16,20},{20,24},{24,28},{1,5},{5,9},{9,... | collective-permute-start | bytes 196616 | tf_op jit(solution)/shard_map/ppermute | solution.py:24
  19.2 5.4 %collective-permute-start.2 = (f32[2,36,2,128]{3,2,1,0:T(2,128)S(1)}, f32[2,36,2,128]{3,2,1,0:T(2,128)S(1)}, u32[]{:S(2)}, u32[]{:S(2)}) collective-permute-start(f32[2,36,2,128]{3,2,1,0:T(2,128)S(1)} %get-tuple-element.90), channel_id=1, source_target_pairs={{1,0},{2,1},{3,2},{5,4},{6,5},{7,6},{9,8},{10,9},{11,10},{13,12},{... | collective-permute-start | bytes 221192 | tf_op jit(solution)/shard_map/ppermute | solution.py:26
  20.5 5.4 %collective-permute-start.3 = (f32[2,36,2,128]{3,2,1,0:T(2,128)S(1)}, f32[2,36,2,128]{3,2,1,0:T(2,128)S(1)}, u32[]{:S(2)}, u32[]{:S(2)}) collective-permute-start(f32[2,36,2,128]{3,2,1,0:T(2,128)S(1)} %get-tuple-element.91), channel_id=1, source_target_pairs={{0,1},{1,2},{2,3},{4,5},{5,6},{6,7},{8,9},{9,10},{10,11},{12,13},{... | collective-permute-start | bytes 221192 | tf_op jit(solution)/shard_map/ppermute | solution.py:24
  30.2 62.8 %copy-start.6 = (f32[131072]{0:T(1024)}, f32[131072]{0:T(1024)S(1)}, u32[]{:S(2)}) copy-start(f32[131072]{0:T(1024)S(1)} %fusion.63) | copy-start | bytes 1572868
  33.7 59.2 %copy-start.2 = (f32[131072]{0:T(1024)}, f32[131072]{0:T(1024)S(1)}, u32[]{:S(2)}) copy-start(f32[131072]{0:T(1024)S(1)} %scatter_fusion) | copy-start | bytes 1572868
  33.8 11.2 %collective-permute-start.4 = (f32[2,2,32,128]{3,2,1,0:T(8,128)S(1)}, f32[2,2,32,128]{3,2,1,0:T(8,128)S(1)}, u32[]{:S(2)}, u32[]{:S(2)}) collective-permute-start(f32[2,2,32,128]{3,2,1,0:T(8,128)S(1)} %get-tuple-element.109), channel_id=1, source_target_pairs={{4,0},{8,4},{12,8},{16,12},{20,16},{24,20},{28,24},{5,1},{9,5},{13... | collective-permute-start | bytes 196616 | tf_op jit(solution)/shard_map/ppermute | solution.py:26
  35.1 9.9 %collective-permute-start.5 = (f32[2,2,32,128]{3,2,1,0:T(8,128)S(1)}, f32[2,2,32,128]{3,2,1,0:T(8,128)S(1)}, u32[]{:S(2)}, u32[]{:S(2)}) collective-permute-start(f32[2,2,32,128]{3,2,1,0:T(8,128)S(1)} %get-tuple-element.108), channel_id=1, source_target_pairs={{0,4},{4,8},{8,12},{12,16},{16,20},{20,24},{24,28},{1,5},{5,9},{9,... | collective-permute-start | bytes 196616 | tf_op jit(solution)/shard_map/ppermute | solution.py:24
  40.2 51.3 %collective-permute-start.12 = (f32[2,8,32,128]{3,2,1,0:T(8,128)}, f32[2,8,32,128]{3,2,1,0:T(8,128)S(1)}, u32[]{:S(2)}, u32[]{:S(2)}) collective-permute-start(f32[2,8,32,128]{3,2,1,0:T(8,128)} %get-tuple-element.96), channel_id=1, source_target_pairs={{0,4},{4,8},{8,12},{12,16},{16,20},{20,24},{24,28},{1,5},{5,9},{9,... | collective-permute-start | bytes 786440 | tf_op jit(solution)/shard_map/ppermute | solution.py:24
  43.7 49.2 %collective-permute-start.13 = (f32[2,8,32,128]{3,2,1,0:T(8,128)}, f32[2,8,32,128]{3,2,1,0:T(8,128)S(1)}, u32[]{:S(2)}, u32[]{:S(2)}) collective-permute-start(f32[2,8,32,128]{3,2,1,0:T(8,128)} %get-tuple-element.97), channel_id=1, source_target_pairs={{4,0},{8,4},{12,8},{16,12},{20,16},{24,20},{28,24},{5,1},{9,5},{13... | collective-permute-start | bytes 786440 | tf_op jit(solution)/shard_map/ppermute | solution.py:26
  45.1 5.9 %collective-permute-start.6 = (f32[2,36,2,128]{3,2,1,0:T(2,128)S(1)}, f32[2,36,2,128]{3,2,1,0:T(2,128)S(1)}, u32[]{:S(2)}, u32[]{:S(2)}) collective-permute-start(f32[2,36,2,128]{3,2,1,0:T(2,128)S(1)} %get-tuple-element.86), channel_id=1, source_target_pairs={{1,0},{2,1},{3,2},{5,4},{6,5},{7,6},{9,8},{10,9},{11,10},{13,12},{... | collective-permute-start | bytes 221192 | tf_op jit(solution)/shard_map/ppermute | solution.py:26
  46.4 5.7 %collective-permute-start.7 = (f32[2,36,2,128]{3,2,1,0:T(2,128)S(1)}, f32[2,36,2,128]{3,2,1,0:T(2,128)S(1)}, u32[]{:S(2)}, u32[]{:S(2)}) collective-permute-start(f32[2,36,2,128]{3,2,1,0:T(2,128)S(1)} %get-tuple-element.87), channel_id=1, source_target_pairs={{0,1},{1,2},{2,3},{4,5},{5,6},{6,7},{8,9},{9,10},{10,11},{12,13},{... | collective-permute-start | bytes 221192 | tf_op jit(solution)/shard_map/ppermute | solution.py:24
  55.9 24.0 %copy-start.8 = (f32[131072]{0:T(1024)}, f32[131072]{0:T(1024)S(1)}, u32[]{:S(2)}) copy-start(f32[131072]{0:T(1024)S(1)} %fusion.64) | copy-start | bytes 1572868
  59.5 20.5 %copy-start.4 = (f32[131072]{0:T(1024)}, f32[131072]{0:T(1024)S(1)}, u32[]{:S(2)}) copy-start(f32[131072]{0:T(1024)S(1)} %scatter_fusion.1) | copy-start | bytes 1572868
  59.6 12.7 %collective-permute-start.8 = (f32[2,2,32,128]{3,2,1,0:T(8,128)S(1)}, f32[2,2,32,128]{3,2,1,0:T(8,128)S(1)}, u32[]{:S(2)}, u32[]{:S(2)}) collective-permute-start(f32[2,2,32,128]{3,2,1,0:T(8,128)S(1)} %get-tuple-element.103), channel_id=1, source_target_pairs={{4,0},{8,4},{12,8},{16,12},{20,16},{24,20},{28,24},{5,1},{9,5},{13... | collective-permute-start | bytes 196616 | tf_op jit(solution)/shard_map/ppermute | solution.py:26
  60.9 11.4 %collective-permute-start.9 = (f32[2,2,32,128]{3,2,1,0:T(8,128)S(1)}, f32[2,2,32,128]{3,2,1,0:T(8,128)S(1)}, u32[]{:S(2)}, u32[]{:S(2)}) collective-permute-start(f32[2,2,32,128]{3,2,1,0:T(8,128)S(1)} %get-tuple-element.102), channel_id=1, source_target_pairs={{0,4},{4,8},{8,12},{12,16},{16,20},{20,24},{24,28},{1,5},{5,9},{9,... | collective-permute-start | bytes 196616 | tf_op jit(solution)/shard_map/ppermute | solution.py:24
  67.8 25.3 %collective-permute-start.14 = (f32[2,8,32,128]{3,2,1,0:T(8,128)}, f32[2,8,32,128]{3,2,1,0:T(8,128)S(1)}, u32[]{:S(2)}, u32[]{:S(2)}) collective-permute-start(f32[2,8,32,128]{3,2,1,0:T(8,128)} %get-tuple-element.94), channel_id=1, source_target_pairs={{0,4},{4,8},{8,12},{12,16},{16,20},{20,24},{24,28},{1,5},{5,9},{9,... | collective-permute-start | bytes 786440 | tf_op jit(solution)/shard_map/ppermute | solution.py:24
  72.4 6.2 %collective-permute-start.10 = (f32[2,36,2,128]{3,2,1,0:T(2,128)S(1)}, f32[2,36,2,128]{3,2,1,0:T(2,128)S(1)}, u32[]{:S(2)}, u32[]{:S(2)}) collective-permute-start(f32[2,36,2,128]{3,2,1,0:T(2,128)S(1)} %get-tuple-element.82), channel_id=1, source_target_pairs={{1,0},{2,1},{3,2},{5,4},{6,5},{7,6},{9,8},{10,9},{11,10},{13,12},{... | collective-permute-start | bytes 221192 | tf_op jit(solution)/shard_map/ppermute | solution.py:26
  73.7 6.2 %collective-permute-start.11 = (f32[2,36,2,128]{3,2,1,0:T(2,128)S(1)}, f32[2,36,2,128]{3,2,1,0:T(2,128)S(1)}, u32[]{:S(2)}, u32[]{:S(2)}) collective-permute-start(f32[2,36,2,128]{3,2,1,0:T(2,128)S(1)} %get-tuple-element.83), channel_id=1, source_target_pairs={{0,1},{1,2},{2,3},{4,5},{5,6},{6,7},{8,9},{9,10},{10,11},{12,13},{... | collective-permute-start | bytes 221192 | tf_op jit(solution)/shard_map/ppermute | solution.py:24
  78.6 14.5 %collective-permute-start.15 = (f32[2,8,32,128]{3,2,1,0:T(8,128)}, f32[2,8,32,128]{3,2,1,0:T(8,128)}, u32[]{:S(2)}, u32[]{:S(2)}) collective-permute-start(f32[2,8,32,128]{3,2,1,0:T(8,128)} %get-tuple-element.95), channel_id=1, source_target_pairs={{4,0},{8,4},{12,8},{16,12},{20,16},{24,20},{28,24},{5,1},{9,5},{13... | collective-permute-start | bytes 786440 | tf_op jit(solution)/shard_map/ppermute | solution.py:26
  87.5 7.3 %collective-permute-start.16 = (f32[2,8,32,128]{3,2,1,0:T(8,128)S(1)}, f32[2,8,32,128]{3,2,1,0:T(8,128)S(1)}, u32[]{:S(2)}, u32[]{:S(2)}) collective-permute-start(f32[2,8,32,128]{3,2,1,0:T(8,128)S(1)} %get-tuple-element.92), channel_id=1, source_target_pairs={{0,4},{4,8},{8,12},{12,16},{16,20},{20,24},{24,28},{1,5},{5,9},{9,... | collective-permute-start | bytes 786440 | tf_op jit(solution)/shard_map/ppermute | solution.py:24
  91.5 8.4 %collective-permute-start.17 = (f32[2,8,32,128]{3,2,1,0:T(8,128)S(1)}, f32[2,8,32,128]{3,2,1,0:T(8,128)S(1)}, u32[]{:S(2)}, u32[]{:S(2)}) collective-permute-start(f32[2,8,32,128]{3,2,1,0:T(8,128)S(1)} %get-tuple-element.93), channel_id=1, source_target_pairs={{4,0},{8,4},{12,8},{16,12},{20,16},{24,20},{28,24},{5,1},{9,5},{13... | collective-permute-start | bytes 786440 | tf_op jit(solution)/shard_map/ppermute | solution.py:26
  253.7 36.4 %copy-start.1 = (s32[32,32]{1,0:T(8,128)S(1)}, s32[32,32]{1,0:T(8,128)}, u32[]{:S(2)}) copy-start(s32[32,32]{1,0:T(8,128)} %param.29) | copy-start | bytes 12292
  (15 other events, 97.3 us)
Sparse Core Ops, SparseCore 0:
  135.0 117.2 all-reduce.5
where the time goes:
time: 300 us; the launch traced here: 297 us
  waiting for transfers between devices  124 us (41%)
  other arithmetic  53.1 us (18%)
  starting transfers between devices  52 us (17%)
  blocking collectives  35.4 us (12%)
  between operations  17.3 us (6%)
  local copies, waits for them, and re-layouts  15.3 us (5%)
    unnamed x2, waiting for transfers between devices  116 us
    ppermute x9, starting transfers between devices, padded(): lax.ppermute(tail, axis, [(i, (i + 1) % count) for i in range(ends)])  40.2 us
    all_to_all x1, blocking collectives, body(): lax.all_to_all(reduced, ('gx', 'gy'), split_axis=1, concat_axis=1, tiled=...  35.4 us
    scatter-add x6, other arithmetic, inject(): flat_field = field_in.reshape(-1).at[flat_index].add(values, mode='drop')  17 us
    cond x14, other arithmetic  16.3 us
    ppermute x9, starting transfers between devices, padded(): lax.ppermute(head, axis, [((i + 1) % count, i) for i in range(ends)])  11.8 us
    select_n x2, other arithmetic, body(): outgoing = jnp.take(strips, strip_for, axis=1)  8.35 us
    gather x1, local copies, waits for them, and re-layouts, body(): outgoing = jnp.take(strips, strip_for, axis=1)  7.72 us
  transfers between devices with their start and end apart: 19, of which 5 were waited for; matrix products, arithmetic and copies ran while one was open for 7% of the time, Pallas kernels for 0%

commit v1 on v0

v1 whole, which is shorter than its diff:
```python
import jax
import jax.numpy as jnp
from jax import lax
from jax.experimental import pallas as pl
from jax.experimental.pallas import tpu as pltpu
from jax.sharding import PartitionSpec as P

MESH = pl.DeviceIdType.MESH
OFFS = 16
STEPS = 3
HALF = 8
NEAR = 4.0 / 3.0
FAR = -1.0 / 12.0
CENTRE = 3.0 * -2.5

CX, CY, NZ = 32, 32, 128
N_GX, N_GY, N_SHOT = 8, 4, 8
TILES = N_GX * N_GY
GROUPS = 4
SG = TILES // GROUPS
CHIPS = N_SHOT // 2
EXT = CX + 2 * HALF
F32 = jnp.float32


def prepare_kernel(pos_ref, data_ref, spos_ref, ap_ref, owner_ref, inj_ref, strip_ref, mask_ref, src_ref):
    gx, gy = lax.axis_index("gx"), lax.axis_index("gy")
    tile = gx * N_GY + gy

    def invert(k, carry):
        strip_ref[owner_ref[tile, k]] = k
        return carry

    lax.fori_loop(0, TILES, invert, 0)
    hit = jnp.int32(0)
    for i in range(ap_ref.shape[1]):
        hit = jnp.where(ap_ref[0, i] == tile, jnp.int32(1), hit)
    mask_ref[0] = hit.astype(F32)
    p = spos_ref[0]
    lx = lax.shift_right_logical(p, 14) - gx * CX
    ly = (lax.shift_right_logical(p, 7) & 127) - gy * CY
    inside = (lx >= 0) & (lx < CX) & (ly >= 0) & (ly < CY)
    src_ref[0] = jnp.where(inside, (lx * CY + ly) * NZ + (p & 127), -1)

    pos = pos_ref[...]
    rx = lax.shift_right_logical(pos, 14) - gx * CX
    ry = (lax.shift_right_logical(pos, 7) & 127) - gy * CY
    rz = pos & 127
    ok = (rx >= 0) & (rx < CX) & (ry >= 0) & (ry < CY)
    cell = jnp.where(ok, rx * CY + ry, -1)
    n = pos.shape[1]
    depth = lax.broadcasted_iota(jnp.int32, (NZ, n), 0) == rz
    parts = [[], [], []]
    for t in range(STEPS):
        left = jnp.where(depth, data_ref[0, t : t + 1, :], 0.0)
        for piece in parts:
            cut = left.astype(jnp.bfloat16)
            piece.append(cut)
            left = left - cut.astype(F32)
    parts = [jnp.concatenate(piece, axis=0) for piece in parts]
    rows = 256
    for first in range(0, CX * CY, rows):
        spot = lax.broadcasted_iota(jnp.int32, (rows, n), 0) + first == cell
        spot = jnp.where(spot, 1.0, 0.0).astype(jnp.bfloat16)
        total = None
        for piece in parts:
            term = lax.dot_general(spot, piece, (((1,), (1,)), ((), ())), preferred_element_type=F32)
            total = term if total is None else total + term
        for t in range(STEPS):
            inj_ref[t, first : first + rows, :] = total[:, t * NZ : (t + 1) * NZ]


def prepare(rcv_pos, rcv_data, src_pos, aperture, owner):
    smem = pl.BlockSpec(memory_space=pltpu.SMEM)
    vmem = pl.BlockSpec(memory_space=pltpu.VMEM)
    return pl.pallas_call(
        prepare_kernel,
        out_shape=(
            jax.ShapeDtypeStruct((STEPS, CX * CY, NZ), F32),
            jax.ShapeDtypeStruct((TILES,), jnp.int32),
            jax.ShapeDtypeStruct((1,), F32),
            jax.ShapeDtypeStruct((1,), jnp.int32),
        ),
        in_specs=[vmem, vmem, smem, smem, smem],
        out_specs=(vmem, smem, smem, smem),
        name="prepare",
    )(rcv_pos, rcv_data, src_pos, aperture, owner)


def main_kernel(
    vel, s_prev, s_cur, r_prev, r_cur, inj, strip, mask, src, amp,
    s_out, r_out, g_out,
    w0, w1, w2, w3, old, speed, drive, ysend, yrecv, part, mate, ring1, ring2, final,
    load_sem, xs_sem, xr_sem, ys_sem, yr_sem, a_sem, b_sem, c_sem, e_sem, out_sem,
):
    gx, gy, shot = lax.axis_index("gx"), lax.axis_index("gy"), lax.axis_index("shot")
    core = lax.rem(shot, 2)
    chip = lax.div(shot, 2)
    tile = gx * N_GY + gy
    fields = (w0, w1, w2, w3)
    has_left, has_right = gx > 0, gx < N_GX - 1
    has_low, has_high = gy > 0, gy < N_GY - 1
    other = {"shot": shot + 1 - 2 * core}
    above = {"shot": lax.rem(shot + 2, N_SHOT)}
    below = {"shot": lax.rem(shot + N_SHOT - 2, N_SHOT)}

    barrier = pltpu.get_barrier_semaphore()
    for peer in (other, above, below):
        pl.semaphore_signal(barrier, inc=1, device_id=peer, device_id_type=MESH)

    def greet(j, carry):
        peer = lax.rem(tile + j, TILES)
        pl.semaphore_signal(
            barrier, inc=1, device_id={"gx": lax.div(peer, N_GY), "gy": lax.rem(peer, N_GY)},
            device_id_type=MESH,
        )
        return carry

    lax.fori_loop(1, TILES, greet, 0)

    inner = (slice(HALF, HALF + CX), slice(HALF, HALF + CY))
    loads = [
        pltpu.make_async_copy(s_cur.at[0], w0.at[(0,) + inner], load_sem.at[0]),
        pltpu.make_async_copy(r_cur.at[0], w0.at[(1,) + inner], load_sem.at[1]),
        pltpu.make_async_copy(s_prev.at[0], old.at[0], load_sem.at[2]),
        pltpu.make_async_copy(r_prev.at[0], old.at[1], load_sem.at[3]),
        pltpu.make_async_copy(vel, speed, load_sem.at[4]),
        pltpu.make_async_copy(inj, drive, load_sem.at[5]),
    ]
    for copy in loads:
        copy.start()

    def clear_x(first, count):
        for w in fields:
            lo, n = (first, count) if w is not w0 else ((6, 2) if first == 0 else (40, 2))

            def body(i, carry, w=w, lo=lo):
                w[0, lo + i, HALF : HALF + CY, :] = jnp.zeros((CY, NZ), F32)
                w[1, lo + i, HALF : HALF + CY, :] = jnp.zeros((CY, NZ), F32)
                return carry

            lax.fori_loop(0, n, body, 0)

    def clear_y(first):
        for w in fields[:STEPS]:

            def body(i, carry, w=w):
                w[0, HALF + i, first : first + 8, :] = jnp.zeros((8, NZ), F32)
                w[1, HALF + i, first : first + 8, :] = jnp.zeros((8, NZ), F32)
                return carry

            lax.fori_loop(0, CX, body, 0)

    pl.when(jnp.logical_not(has_left))(lambda: clear_x(0, HALF))
    pl.when(jnp.logical_not(has_right))(lambda: clear_x(HALF + CX, HALF))
    pl.when(jnp.logical_not(has_low))(lambda: clear_y(0))
    pl.when(jnp.logical_not(has_high))(lambda: clear_y(HALF + CY))

    def x_copy(t, way, piece):
        w = fields[t]
        if way == 0:
            here, there = ((38, 6), (32, 0))[piece]
            to = {"gx": gx + 1}
        else:
            here, there = ((8, 40), (10, 42))[piece]
            to = {"gx": gx - 1}
        n = (2, 6)[piece]
        return pltpu.make_async_remote_copy(
            src_ref=w.at[:, here : here + n, HALF : HALF + CY, :],
            dst_ref=w.at[:, there : there + n, HALF : HALF + CY, :],
            send_sem=xs_sem.at[t, way, piece],
            recv_sem=xr_sem.at[t, way, piece],
            device_id=to,
            device_id_type=MESH,
        )

    def y_copy(t, way):
        return pltpu.make_async_remote_copy(
            src_ref=ysend.at[t, way],
            dst_ref=yrecv.at[t, way],
            send_sem=ys_sem.at[t, way],
            recv_sem=yr_sem.at[t, way],
            device_id={"gy": gy + 1 - 2 * way},
            device_id_type=MESH,
        )

    x_to = (has_right, has_left)
    x_from = (has_left, has_right)
    y_to = (has_high, has_low)
    y_from = (has_low, has_high)

    def send_x(t, piece):
        for way in range(2):
            pl.when(x_to[way])(lambda: x_copy(t, way, piece).start())

    def got_x(t, piece):
        for way in range(2):
            pl.when(x_from[way])(lambda: x_copy(t, way, piece).wait_recv())

    def pack_y(t):
        w = fields[t]

        def body(i, carry):
            for f in range(2):
                for j in range(4):
                    row = pl.ds(f * 2 * CX + pl.multiple_of(i * 8, 8) + 2 * j, 2)
                    ysend[t, 0, row, :] = w[f, HALF + i * 4 + j, HALF + CY - 2 : HALF + CY, :]
                    ysend[t, 1, row, :] = w[f, HALF + i * 4 + j, HALF : HALF + 2, :]
            return carry

        lax.fori_loop(0, CX // 4, body, 0)

    def unpack_y(t, way):
        w = fields[t]
        at = HALF - 2 if way == 0 else HALF + CY

        def body(i, carry):
            for f in range(2):
                for j in range(4):
                    row = pl.ds(f * 2 * CX + pl.multiple_of(i * 8, 8) + 2 * j, 2)
                    w[f, HALF + i * 4 + j, at : at + 2, :] = yrecv[t, way, row, :]
            return carry

        lax.fori_loop(0, CX // 4, body, 0)

    def send_y(t):
        pack_y(t)
        for way in range(2):
            pl.when(y_to[way])(lambda: y_copy(t, way).start())

    def got_y(t):
        for way in range(2):

            def body(way=way):
                y_copy(t, way).wait_recv()
                unpack_y(t, way)

            pl.when(y_from[way])(body)

    lane = lax.broadcasted_iota(jnp.int32, (8, NZ), 1)
    near_up = jnp.where(lane < NZ - 1, NEAR, 0.0)
    near_down = jnp.where(lane > 0, NEAR, 0.0)
    far_up = jnp.where(lane < NZ - 2, FAR, 0.0)
    far_down = jnp.where(lane > 1, FAR, 0.0)
    spot = lax.broadcasted_iota(jnp.int32, (8, NZ), 0) * NZ + lane

    def advance(t):
        w, new = fields[t], fields[t + 1]
        where = src[0]
        push = amp[0, t]

        def body(x, carry):
            X = x + HALF
            for y in range(CY // 8):
                Y = HALF + 8 * y
                v = speed[x, 8 * y : 8 * y + 8, :]
                for f in range(2):
                    c = w[f, X, Y : Y + 8, :]
                    lap = CENTRE * c
                    lap = lap + NEAR * (w[f, X + 1, Y : Y + 8, :] + w[f, X - 1, Y : Y + 8, :])
                    lap = lap + FAR * (w[f, X + 2, Y : Y + 8, :] + w[f, X - 2, Y : Y + 8, :])
                    lap = lap + NEAR * (w[f, X, Y + 1 : Y + 9, :] + w[f, X, Y - 1 : Y + 7, :])
                    lap = lap + FAR * (w[f, X, Y + 2 : Y + 10, :] + w[f, X, Y - 2 : Y + 6, :])
                    lap = lap + near_up * pltpu.roll(c, NZ - 1, 1) + near_down * pltpu.roll(c, 1, 1)
                    lap = lap + far_up * pltpu.roll(c, NZ - 2, 1) + far_down * pltpu.roll(c, 2, 1)
                    if t == 0:
                        before = old[f, x, 8 * y : 8 * y + 8, :]
                    else:
                        before = fields[t - 1][f, X, Y : Y + 8, :]
                    value = 2.0 * c - before + v * lap
                    if f == 0:
                        add = jnp.where(spot == where - (x * CY + 8 * y) * NZ, push, 0.0)
                    else:
                        add = drive[t, pl.ds(pl.multiple_of(x * CY + 8 * y, 8), 8), :]
                    new[f, X, Y : Y + 8, :] = value + add
            return carry

        lax.fori_loop(0, CX, body, 0)

    for copy in loads[:2]:
        copy.wait()
    pl.semaphore_wait(barrier, TILES - 1 + 3)
    send_x(0, 0)
    send_y(0)
    for copy in loads[2:]:
        copy.wait()
    for t in range(STEPS):
        got_x(t, 0)
        got_y(t)
        advance(t)
        send_x(t + 1, 0)
        if t + 1 < STEPS:
            send_y(t + 1)
        send_x(t + 1, 1)

    store_s = pltpu.make_async_copy(w3.at[(0,) + inner], s_out.at[0], out_sem.at[0])
    store_r = pltpu.make_async_copy(w3.at[(1,) + inner], r_out.at[0], out_sem.at[1])
    store_s.start()
    store_r.start()

    got_x(STEPS, 0)
    for t in range(1, STEPS + 1):
        got_x(t, 1)

    m = mask[0]
    dxs = (2, 1, 3, 0)
    dzs = (4, 3, 5, 2, 6, 1, 7, 0)

    def to_whom(group, i):
        dx = jnp.int32(dxs[0])
        for g in range(1, GROUPS):
            dx = jnp.where(group == g, dxs[g], dx)
        dz = jnp.int32(dzs[0])
        for j in range(1, SG):
            dz = jnp.where(i == j, dzs[j], dz)
        return lax.rem(gx + dz, N_GX), lax.rem(gy + dx, N_GY)

    def correlate(group):
        def body(i, carry):
            ox, oy = to_whom(group, i)
            k = strip[ox * N_GY + oy]
            for y in range(CY // 8):
                Y = HALF + 8 * y
                for h in range(OFFS):
                    total = None
                    for w in (w1, w2, w3):
                        term = w[0, k + OFFS - h, Y : Y + 8, :] * w[1, k + h, Y : Y + 8, :]
                        total = term if total is None else total + term
                    away = lax.rem((h // 2) % 2 + core, 2)
                    part[away, group, h // 4, h % 2, i, 8 * y : 8 * y + 8, :] = total * m
            return carry

        lax.fori_loop(0, SG, body, 0)

    def a_copy(group):
        return pltpu.make_async_remote_copy(
            src_ref=part.at[1, group], dst_ref=mate.at[group],
            send_sem=a_sem.at[0, group], recv_sem=a_sem.at[1, group],
            device_id=other, device_id_type=MESH,
        )

    def b_copy(group, way):
        return pltpu.make_async_remote_copy(
            src_ref=part.at[0, group, lax.rem(chip + 2, CHIPS), way], dst_ref=ring1.at[group, way],
            send_sem=b_sem.at[0, group, way], recv_sem=b_sem.at[1, group, way],
            device_id=(above, below)[way], device_id_type=MESH,
        )

    def c_copy(group, way):
        return pltpu.make_async_remote_copy(
            src_ref=part.at[0, group, lax.rem(chip + (1, 3)[way], CHIPS)], dst_ref=ring2.at[group, way],
            send_sem=c_sem.at[0, group, way], recv_sem=c_sem.at[1, group, way],
            device_id=(above, below)[way], device_id_type=MESH,
        )

    def e_copy(group, i):
        ox, oy = to_whom(group, i)
        return pltpu.make_async_remote_copy(
            src_ref=final.at[group * SG + i], dst_ref=g_out.at[0, :, tile, 0],
            send_sem=e_sem.at[0], recv_sem=e_sem.at[1],
            device_id={"gx": ox, "gy": oy}, device_id_type=MESH,
        )

    def own_copy():
        return pltpu.make_async_copy(final.at[TILES - 1], g_out.at[0, :, tile, 0], e_sem.at[2])

    def add_mate(group, which):
        def body(i, carry):
            for h in range(2):
                part[0, group, which, h, i] = part[0, group, which, h, i] + mate[group, which, h, i]
            return carry

        lax.fori_loop(0, SG, body, 0)

    def from_mate(group):
        a_copy(group).wait_recv()
        add_mate(group, lax.rem(chip + 2, CHIPS))
        for way in range(2):
            b_copy(group, way).start()
        for far in (1, 3, 0):
            add_mate(group, lax.rem(chip + far, CHIPS))

    def from_ring1(group):
        for way in range(2):
            b_copy(group, way).wait_recv()
            which = lax.rem(chip + (1, 3)[way], CHIPS)

            def body(i, carry):
                part[0, group, which, way, i] = part[0, group, which, way, i] + ring1[group, way, i]
                return carry

            lax.fori_loop(0, SG, body, 0)
            c_copy(group, way).start()

    def from_ring2(group):
        for way in range(2):
            c_copy(group, way).wait_recv()

        def body(i, carry):
            for h in range(2):
                final[group * SG + i, h] = (
                    part[0, group, chip, h, i] + ring2[group, 0, h, i] + ring2[group, 1, h, i]
                )
            mine = (group == GROUPS - 1) & (i == SG - 1)

            @pl.when(mine)
            def _():
                own_copy().start()

            @pl.when(jnp.logical_not(mine))
            def _():
                e_copy(group, i).start()

            return carry

        lax.fori_loop(0, SG, body, 0)

    def stage(it, carry):
        @pl.when(it < GROUPS)
        def _():
            correlate(it)
            a_copy(it).start()

        @pl.when((it >= 1) & (it < GROUPS + 1))
        def _():
            from_mate(it - 1)

        @pl.when((it >= 2) & (it < GROUPS + 2))
        def _():
            from_ring1(it - 2)

        @pl.when(it >= 3)
        def _():
            from_ring2(it - 3)

        return carry

    lax.fori_loop(0, GROUPS + 3, stage, 0)

    for t in range(STEPS + 1):
        for way in range(2):
            for piece in range(2 if t else 1):
                pl.when(x_to[way])(lambda: x_copy(t, way, piece).wait_send())
    for t in range(STEPS):
        for way in range(2):
            pl.when(y_to[way])(lambda: y_copy(t, way).wait_send())

    def drain(group, carry):
        a_copy(group).wait_send()
        for way in range(2):
            b_copy(group, way).wait_send()
            c_copy(group, way).wait_send()
        return carry

    lax.fori_loop(0, GROUPS, drain, 0)
    store_s.wait()
    store_r.wait()
    own_copy().wait()
    pltpu.make_async_copy(final.at[0 : TILES - 1], final.at[0 : TILES - 1], e_sem.at[0]).wait()
    arrived = g_out.at[0, :, 0 : TILES - 1, 0]
    pltpu.make_async_copy(arrived, arrived, e_sem.at[1]).wait()


def body(vel_coef, src_prev, src_cur, rcv_prev, rcv_cur, src_pos, src_amp, rcv_pos, rcv_data, aperture, owner):
    inj, strip, mask, src = prepare(rcv_pos, rcv_data, src_pos, aperture, owner)
    whole = pl.BlockSpec(memory_space=pl.ANY)
    smem = pl.BlockSpec(memory_space=pltpu.SMEM)
    DMA = pltpu.SemaphoreType.DMA
    wave = pltpu.VMEM((2, EXT, CY + 16, NZ), F32)
    return pl.pallas_call(
        main_kernel,
        out_shape=(
            jax.ShapeDtypeStruct(src_cur.shape, F32),
            jax.ShapeDtypeStruct(rcv_cur.shape, F32),
            jax.ShapeDtypeStruct((1, 2, TILES, 1, CY, NZ), F32),
        ),
        in_specs=[whole] * 6 + [smem] * 4,
        out_specs=(whole, whole, whole),
        scratch_shapes=[
            wave, wave, wave, wave,
            pltpu.VMEM((2, CX, CY, NZ), F32),
            pltpu.VMEM((CX, CY, NZ), F32),
            pltpu.VMEM((STEPS, CX * CY, NZ), F32),
            pltpu.VMEM((STEPS, 2, 4 * CX, NZ), F32),
            pltpu.VMEM((STEPS, 2, 4 * CX, NZ), F32),
            pltpu.VMEM((2, GROUPS, CHIPS, 2, SG, CY, NZ), F32),
            pltpu.VMEM((GROUPS, CHIPS, 2, SG, CY, NZ), F32),
            pltpu.VMEM((GROUPS, 2, SG, CY, NZ), F32),
            pltpu.VMEM((GROUPS, 2, 2, SG, CY, NZ), F32),
            pltpu.VMEM((TILES, 2, CY, NZ), F32),
            DMA((6,)),
            DMA((STEPS + 1, 2, 2)),
            DMA((STEPS + 1, 2, 2)),
            DMA((STEPS, 2)),
            DMA((STEPS, 2)),
            DMA((2, GROUPS)),
            DMA((2, GROUPS, 2)),
            DMA((2, GROUPS, 2)),
            DMA((3,)),
            DMA((2,)),
        ],
        compiler_params=pltpu.CompilerParams(
            collective_id=0, has_side_effects=True, vmem_limit_bytes=48 * 1024 * 1024
        ),
        name="migrate",
    )(vel_coef, src_prev, src_cur, rcv_prev, rcv_cur, inj, strip, mask, src, src_amp)


def solution(mesh):
    return jax.shard_map(
        body,
        mesh=mesh,
        in_specs=(
            P("gx", "gy", None),
            P("shot", "gx", "gy", None),
            P("shot", "gx", "gy", None),
            P("shot", "gx", "gy", None),
            P("shot", "gx", "gy", None),
            P("shot"),
            P("shot", None),
            P("shot", None),
            P("shot", None, None),
            P("shot", None),
            P(),
        ),
        out_specs=(
            P("shot", "gx", "gy", None),
            P("shot", "gx", "gy", None),
            P(("gx", "gy"), "shot", None, None, None, None),
        ),
        check_vma=False,
    )
```

time: 300 us -> 106 us (0.35)
  waiting for transfers between devices: 124 us -> 0 us
  Pallas kernels: 0 us -> 93.5 us
  other arithmetic: 53.1 us -> 0 us
  starting transfers between devices: 52 us -> 0 us
  blocking collectives: 35.4 us -> 0 us
  between operations: 17.3 us -> 1.31 us
  local copies, waits for them, and re-layouts: 15.3 us -> 10.4 us
    unnamed x2 -> x0, waiting for transfers between devices: 116 us -> none
    pallas_call x0 -> x2, Pallas kernels: none -> 93.5 us  [the longest x1 89 us: body(): pl.pallas_call(main_kernel, out_shape=(jax.ShapeDtypeStruct(src_cur.shape...]
    ppermute x18 -> x0, starting transfers between devices: 52 us -> none  [the longest x9 40.2 us: padded(): lax.ppermute(tail, axis, [(i, (i + 1) % count) for i in range(ends)])]
    all_to_all x1 -> x0, blocking collectives: 35.4 us -> none  [body(): lax.all_to_all(reduced, ('gx', 'gy'), split_axis=1, concat_axis=1, tiled=...]
    scatter-add x6 -> x0, other arithmetic: 17 us -> none  [inject(): flat_field = field_in.reshape(-1).at[flat_index].add(values, mode='drop')]
    cond x14 -> x0, other arithmetic: 16.3 us -> none
    select_n x3 -> x0, other arithmetic: 8.4 us -> none  [the longest x2 8.35 us: body(): outgoing = jnp.take(strips, strip_for, axis=1)]
    ppermute x18 -> x0, waiting for transfers between devices: 8.14 us -> none  [the longest x9 5.21 us: padded(): lax.ppermute(head, axis, [((i + 1) % count, i) for i in range(ends)])]
  transfers between devices with their start and end apart: 19 -> 0, of which waited for: 5 -> 0; matrix products, arithmetic and copies ran while one was open for 7% -> 0% of each run, Pallas kernels for 0% -> 0%
where the time goes in v1:
time: 106 us; the launch traced here: 105 us
  Pallas kernels  93.5 us (88%)
  local copies, waits for them, and re-layouts  10.4 us (10%)
  between operations  1.31 us (1%)
    pallas_call x1, Pallas kernels, body(): pl.pallas_call(main_kernel, out_shape=(jax.ShapeDtypeStruct(src_cur.shape...  89 us
    unnamed x18, local copies, waits for them, and re-layouts  10.4 us
    pallas_call x1, Pallas kernels, prepare(): pl.pallas_call(prepare_kernel, out_shape=(jax.ShapeDtypeStruct((STEPS, CX...  4.46 us

profile of v1, /device:TPU:1, one launch (start us, length us, event | category | flops | bytes accessed | tf_op | source)
XLA Modules:
  0.0 105.2 jit_solution(7194495598828692964)
XLA Ops:
  1.3 1.3 %copy.14.data_ref = f32[1,3,512]{2,1,0:T(4,128)} copy(f32[1,3,512]{2,0,1:T(1,128)} %param.19) | data formatting | bytes 12288 | tf_op args[8]
  2.6 4.5 %prepare.1 = (f32[3,1024,128]{2,1,0:T(8,128)}, s32[32]{0:T(128)}, f32[1]{0:T(128)}, s32[1]{0:T(128)}) custom-call(s32[1,512]{1,0:T(1,128)} %pos_ref.1, f32[1,3,512]{2,1,0:T(4,128)} %copy.14.data_ref, s32[1]{0:T(128)S(6)} %copy.18.spos_ref, s32[1,16]{1,0:T(1,128)} %ap_ref.1, s32[32,32]{1,0:T(8,128)} %owner_ref.1), custom_call_target="tpu_custom_call" | custom-call | tf_op jit(solution)/shard_map/prepare/pallas_call | solution.py:76
  7.0 0.0 copy-start
  7.0 1.0 copy-done
  8.1 0.0 copy-start.1
  8.1 1.0 copy-done.1
  9.1 0.0 copy-start.2
  9.1 1.0 copy-done.2
  10.2 0.0 copy-start.3
  10.2 1.0 copy-done.3
  11.2 0.0 copy-start.4
  11.2 1.0 copy-done.4
  12.2 0.0 copy-start.5
  12.3 0.7 copy-done.5
  12.9 0.0 copy-start.6
  12.9 0.7 copy-done.6
  13.6 89.0 %migrate.1 = (f32[1,32,32,128]{3,2,1,0:T(8,128)S(1)}, f32[1,32,32,128]{3,2,1,0:T(8,128)S(1)}, f32[1,2,32,1,32,128]{5,4,3,2,1,0:T(8,128)S(1)}) custom-call(f32[32,32,128]{2,1,0:T(8,128)S(1)} %copy-done, f32[1,32,32,128]{3,2,1,0:T(8,128)S(1)} %copy-done.1, f32[1,32,32,128]{3,2,1,0:T(8,128)S(1)} %copy-done.2, f32[1,32,32,128]{3,2,1,0:T(8,128)S(1)} %copy-done.3, ...), custom_call_target="tpu_custom_call" | custom-call | tf_op jit(solution)/shard_map/migrate/pallas_call | solution.py:470
  102.6 0.8 copy.19
  103.4 0.8 copy.20
  104.2 1.0 copy.21
Async XLA Ops:
  7.0 1.0 copy-start
  8.1 1.0 copy-start.1
  9.1 1.0 copy-start.2
  10.2 1.0 copy-start.3
  11.2 1.0 copy-start.4
  12.2 0.7 copy-start.5
  12.9 0.7 copy-start.6

commit v2 on v1

v2 whole, which is shorter than its diff:
```python
import jax
import jax.numpy as jnp
from jax import lax
from jax.experimental import pallas as pl
from jax.experimental.pallas import tpu as pltpu
from jax.sharding import PartitionSpec as P

MESH = pl.DeviceIdType.MESH
OFFS = 16
STEPS = 3
HALF = 8
NEAR = 4.0 / 3.0
FAR = -1.0 / 12.0
CENTRE = 3.0 * -2.5

CX, CY, NZ = 32, 32, 128
N_GX, N_GY, N_SHOT = 8, 4, 8
TILES = N_GX * N_GY
GROUPS = 4
SG = TILES // GROUPS
CHIPS = N_SHOT // 2
EDGE = 2
EXT = CX + 2 * HALF
BAND = 8
F32 = jnp.float32


def main_kernel(
    vel, s_prev, s_cur, r_prev, r_cur, pos_ref, data_ref, ap_ref, owner_ref, spos, amp,
    s_out, r_out, g_out,
    w0, w1, w2, w3, bands, old, speed, drive, ysend, yrecv, part, half, final, masks, strip_v, strip,
    load_sem, xs_sem, xr_sem, ys_sem, yr_sem, ms_sem, mr_sem, es_sem, er_sem, zs_sem, zr_sem,
    bs_sem, br_sem, cs_sem, cr_sem, d_sem, out_sem,
):
    gx, gy, shot = lax.axis_index("gx"), lax.axis_index("gy"), lax.axis_index("shot")
    core = lax.rem(shot, 2)
    chip = lax.div(shot, 2)
    tile = gx * N_GY + gy
    fields = (w0, w1, w2, w3)
    has_left, has_right = gx > 0, gx < N_GX - 1
    has_low, has_high = gy > 0, gy < N_GY - 1

    def pair_a(c):
        return c + 1 - 2 * lax.rem(c, 2)

    def pair_b(c):
        return CHIPS - 1 - c

    def band_a(c):
        return lax.rem(lax.div(c + 1, 2), 2)

    def band_b(c):
        return 2 + lax.div(c, 2)

    chip_a, chip_b = pair_a(chip), pair_b(chip)
    first = jnp.where(core == 0, chip_a, chip_b)
    second = jnp.where(core == 0, chip_b, chip_a)
    band = jnp.where(core == 0, band_a(chip), band_b(chip))
    mate = {"shot": shot + 1 - 2 * core}
    peers = (mate, {"shot": 2 * chip_a}, {"shot": 2 * chip_a + 1}, {"shot": 2 * chip_b}, {"shot": 2 * chip_b + 1})

    barrier = pltpu.get_barrier_semaphore()
    for peer in peers:
        pl.semaphore_signal(barrier, inc=1, device_id=peer, device_id_type=MESH)

    def greet(j, carry):
        peer = lax.rem(tile + j, TILES)
        pl.semaphore_signal(
            barrier, inc=1, device_id={"gx": lax.div(peer, N_GY), "gy": lax.rem(peer, N_GY)},
            device_id_type=MESH,
        )
        return carry

    lax.fori_loop(1, TILES, greet, 0)

    inner = (slice(EDGE, EDGE + CX), slice(8, 8 + CY))
    loads = [
        pltpu.make_async_copy(s_cur.at[0], w0.at[(0,) + inner], load_sem.at[0]),
        pltpu.make_async_copy(r_cur.at[0], w0.at[(1,) + inner], load_sem.at[1]),
        pltpu.make_async_copy(s_prev.at[0], old.at[0], load_sem.at[2]),
        pltpu.make_async_copy(r_prev.at[0], old.at[1], load_sem.at[3]),
        pltpu.make_async_copy(vel, speed, load_sem.at[4]),
    ]
    for copy in loads:
        copy.start()

    row = owner_ref[pl.ds(tile, 1), :]
    match = row == lax.broadcasted_iota(jnp.int32, (TILES, TILES), 0)
    number = lax.broadcasted_iota(jnp.int32, (TILES, TILES), 1)
    found = jnp.max(jnp.where(match, number, 0), axis=1, keepdims=True)
    strip_v[...] = jnp.broadcast_to(found, (TILES, NZ))
    table = pltpu.make_async_copy(strip_v, strip, load_sem.at[5])
    table.start()
    hit = jnp.max(jnp.where(ap_ref[...] == tile, 1.0, 0.0), axis=1, keepdims=True)
    masks[0] = jnp.broadcast_to(hit, (8, NZ))

    def clear_x(at, wide):
        def body(i, carry):
            for w in fields[:STEPS]:
                for f in range(2):
                    w[f, at + i, 8 : 8 + CY, :] = jnp.zeros((CY, NZ), F32)
            return carry

        lax.fori_loop(0, EDGE, body, 0)

        def body2(i, carry):
            for t in range(STEPS):
                for s in range(4):
                    for f in range(2):
                        bands[t, s, f, wide + i] = jnp.zeros((BAND, NZ), F32)
            return carry

        lax.fori_loop(0, HALF, body2, 0)

    def clear_y(at):
        def body(i, carry):
            for w in fields[:STEPS]:
                for f in range(2):
                    w[f, EDGE + i, at : at + 8, :] = jnp.zeros((8, NZ), F32)
            return carry

        lax.fori_loop(0, CX, body, 0)

    pl.when(jnp.logical_not(has_left))(lambda: clear_x(0, 0))
    pl.when(jnp.logical_not(has_right))(lambda: clear_x(EDGE + CX, HALF + CX))
    pl.when(jnp.logical_not(has_low))(lambda: clear_y(0))
    pl.when(jnp.logical_not(has_high))(lambda: clear_y(8 + CY))

    def inject():
        pos = pos_ref[...]
        rx = lax.shift_right_logical(pos, 14) - gx * CX
        ry = (lax.shift_right_logical(pos, 7) & 127) - gy * CY
        ok = (rx >= 0) & (rx < CX) & (ry >= 0) & (ry < CY)
        cell = jnp.where(ok, rx * CY + ry, -1)
        n = pos.shape[1]
        depth = lax.broadcasted_iota(jnp.int32, (NZ, n), 0) == (pos & 127)
        parts = [[], [], []]
        for t in range(STEPS):
            left = jnp.where(depth, data_ref[t], 0.0)
            for piece in parts:
                cut = left.astype(jnp.bfloat16)
                piece.append(cut)
                left = left - cut.astype(F32)
        parts = [jnp.concatenate(piece, axis=0) for piece in parts]
        rows = 256
        for at in range(0, CX * CY, rows):
            spot = lax.broadcasted_iota(jnp.int32, (rows, n), 0) + at == cell
            spot = jnp.where(spot, 1.0, 0.0).astype(jnp.bfloat16)
            total = None
            for piece in parts:
                term = lax.dot_general(spot, piece, (((1,), (1,)), ((), ())), preferred_element_type=F32)
                total = term if total is None else total + term
            for t in range(STEPS):
                drive[t, at : at + rows, :] = total[:, t * NZ : (t + 1) * NZ]

    inject()

    def x_copy(t, way):
        here, there = ((CX, 0), (EDGE, EDGE + CX))[way]
        return pltpu.make_async_remote_copy(
            src_ref=fields[t].at[:, here : here + EDGE, 8 : 8 + CY, :],
            dst_ref=fields[t].at[:, there : there + EDGE, 8 : 8 + CY, :],
            send_sem=xs_sem.at[t, way], recv_sem=xr_sem.at[t, way],
            device_id={"gx": gx + 1 - 2 * way}, device_id_type=MESH,
        )

    def y_copy(t, way):
        return pltpu.make_async_remote_copy(
            src_ref=ysend.at[t, way], dst_ref=yrecv.at[t, way],
            send_sem=ys_sem.at[t, way], recv_sem=yr_sem.at[t, way],
            device_id={"gy": gy + 1 - 2 * way}, device_id_type=MESH,
        )

    x_to, x_from = (has_right, has_left), (has_left, has_right)
    y_to, y_from = (has_high, has_low), (has_low, has_high)

    def send_x(t):
        for way in range(2):
            pl.when(x_to[way])(lambda: x_copy(t, way).start())

    def got_x(t):
        for way in range(2):
            pl.when(x_from[way])(lambda: x_copy(t, way).wait_recv())

    def y_rows(i, f, j):
        return pl.ds(f * 2 * CX + pl.multiple_of(i * 8, 8) + 2 * j, 2)

    def send_y(t):
        w = fields[t]

        def body(i, carry):
            for f in range(2):
                for j in range(4):
                    ysend[t, 0, y_rows(i, f, j), :] = w[f, EDGE + i * 4 + j, 6 + CY : 8 + CY, :]
                    ysend[t, 1, y_rows(i, f, j), :] = w[f, EDGE + i * 4 + j, 8:10, :]
            return carry

        lax.fori_loop(0, CX // 4, body, 0)
        for way in range(2):
            pl.when(y_to[way])(lambda: y_copy(t, way).start())

    def got_y(t):
        w = fields[t]
        for way in range(2):
            at = (6, 8 + CY)[way]

            def take(way=way, at=at):
                y_copy(t, way).wait_recv()

                def body(i, carry):
                    for f in range(2):
                        for j in range(4):
                            w[f, EDGE + i * 4 + j, at : at + 2, :] = yrecv[t, way, y_rows(i, f, j), :]
                    return carry

                lax.fori_loop(0, CX // 4, body, 0)

            pl.when(y_from[way])(take)

    targets = (
        (mate, 1, jnp.where(core == 0, band_b(chip), band_a(chip))),
        ({"shot": 2 * chip_a}, 2 + core, band_a(chip_a)),
        ({"shot": 2 * chip_b + 1}, 2 + core, band_b(chip_b)),
    )
    cuts = ((0, 8), (CX - 8, 8), (8, CX - 16))

    def m_copy(target):
        to, slot, _ = targets[target]
        return pltpu.make_async_remote_copy(
            src_ref=masks.at[0], dst_ref=masks.at[slot],
            send_sem=ms_sem.at[target], recv_sem=mr_sem.at[slot - 1],
            device_id=to, device_id_type=MESH,
        )

    def m_arrival(slot):
        return pltpu.make_async_copy(masks.at[slot], masks.at[slot], mr_sem.at[slot - 1])

    def band_rows(b):
        return pl.ds(pl.multiple_of(8 + BAND * b, 8), BAND)

    def e_copy(t, target, cut):
        to, slot, b = targets[target]
        at, n = cuts[cut]
        return pltpu.make_async_remote_copy(
            src_ref=fields[t].at[:, EDGE + at : EDGE + at + n, band_rows(b), :],
            dst_ref=bands.at[t - 1, slot, :, HALF + at : HALF + at + n],
            send_sem=es_sem.at[t - 1, target, cut], recv_sem=er_sem.at[t - 1, slot - 1, cut],
            device_id=to, device_id_type=MESH,
        )

    def e_arrival(t, slot, cut):
        at, n = cuts[cut]
        ref = bands.at[t - 1, slot, :, HALF + at : HALF + at + n]
        return pltpu.make_async_copy(ref, ref, er_sem.at[t - 1, slot - 1, cut])

    def e_own(t):
        return pltpu.make_async_copy(
            fields[t].at[:, EDGE : EDGE + CX, band_rows(band), :],
            bands.at[t - 1, 0, :, HALF : HALF + CX],
            es_sem.at[t - 1, 3, 0],
        )

    def send_e(t):
        e_own(t).start()
        for cut in range(3):
            for target in (1, 2, 0):
                e_copy(t, target, cut).start()

    def z_copy(t, way, f):
        here, there, n = (
            ((CX + 1, 1, HALF - 1), (CX, 0, HALF)),
            ((HALF, HALF + CX, HALF), (HALF, HALF + CX, HALF - 1)),
        )[way][f]
        return pltpu.make_async_remote_copy(
            src_ref=bands.at[t - 1, :, f, here : here + n],
            dst_ref=bands.at[t - 1, :, f, there : there + n],
            send_sem=zs_sem.at[t - 1, way, f], recv_sem=zr_sem.at[t - 1, way, f],
            device_id={"gx": gx + 1 - 2 * way}, device_id_type=MESH,
        )

    def send_z(t):
        e_own(t).wait()
        for slot in range(1, 4):
            for cut in range(2):
                e_arrival(t, slot, cut).wait()
        for way in range(2):
            for f in range(2):
                pl.when(x_to[way])(lambda: z_copy(t, way, f).start())

    lane = lax.broadcasted_iota(jnp.int32, (8, NZ), 1)
    near_up = jnp.where(lane < NZ - 1, NEAR, 0.0)
    near_down = jnp.where(lane > 0, NEAR, 0.0)
    far_up = jnp.where(lane < NZ - 2, FAR, 0.0)
    far_down = jnp.where(lane > 1, FAR, 0.0)
    spot = lax.broadcasted_iota(jnp.int32, (8, NZ), 0) * NZ + lane
    p = spos[0]
    lx = lax.shift_right_logical(p, 14) - gx * CX
    ly = (lax.shift_right_logical(p, 7) & 127) - gy * CY
    inside = (lx >= 0) & (lx < CX) & (ly >= 0) & (ly < CY)
    where = jnp.where(inside, (lx * CY + ly) * NZ + (p & 127), -1)

    def advance(t):
        w, new = fields[t], fields[t + 1]
        push = amp[0, t]

        def body(x, carry):
            X = x + EDGE
            for y in range(CY // 8):
                Y = 8 + 8 * y
                v = speed[x, 8 * y : 8 * y + 8, :]
                for f in range(2):
                    c = w[f, X, Y : Y + 8, :]
                    lap = CENTRE * c
                    lap = lap + NEAR * (w[f, X + 1, Y : Y + 8, :] + w[f, X - 1, Y : Y + 8, :])
                    lap = lap + FAR * (w[f, X + 2, Y : Y + 8, :] + w[f, X - 2, Y : Y + 8, :])
                    lap = lap + NEAR * (w[f, X, Y + 1 : Y + 9, :] + w[f, X, Y - 1 : Y + 7, :])
                    lap = lap + FAR * (w[f, X, Y + 2 : Y + 10, :] + w[f, X, Y - 2 : Y + 6, :])
                    lap = lap + near_up * pltpu.roll(c, NZ - 1, 1) + near_down * pltpu.roll(c, 1, 1)
                    lap = lap + far_up * pltpu.roll(c, NZ - 2, 1) + far_down * pltpu.roll(c, 2, 1)
                    if t == 0:
                        before = old[f, x, 8 * y : 8 * y + 8, :]
                    else:
                        before = fields[t - 1][f, X, Y : Y + 8, :]
                    value = 2.0 * c - before + v * lap
                    if f == 0:
                        add = jnp.where(spot == where - (x * CY + 8 * y) * NZ, push, 0.0)
                    else:
                        add = drive[t, pl.ds(pl.multiple_of(x * CY + 8 * y, 8), 8), :]
                    new[f, X, Y : Y + 8, :] = value + add
            return carry

        lax.fori_loop(0, CX, body, 0)

    for copy in loads[:2]:
        copy.wait()
    pl.semaphore_wait(barrier, TILES - 1 + len(peers))
    send_x(0)
    send_y(0)
    for target in range(3):
        m_copy(target).start()
    for copy in loads[2:]:
        copy.wait()
    table.wait()
    for t in range(STEPS):
        got_x(t)
        got_y(t)
        advance(t)
        if t + 1 < STEPS:
            send_x(t + 1)
            send_y(t + 1)
        send_e(t + 1)
        if t:
            send_z(t)
    stores = [
        pltpu.make_async_copy(w3.at[(f,) + inner], (s_out, r_out)[f].at[0], out_sem.at[f]) for f in range(2)
    ]
    for copy in stores:
        copy.start()
    send_z(STEPS)
    for slot in range(1, 4):
        m_arrival(slot).wait()
    for t in range(1, STEPS + 1):
        for slot in range(1, 4):
            e_arrival(t, slot, 2).wait()
    for t in range(1, STEPS + 1):
        for way in range(2):
            for f in range(2):
                pl.when(x_from[way])(lambda: z_copy(t, way, f).wait_recv())

    dxs = (2, 1, 3, 0)
    dzs = (4, 3, 5, 2, 6, 1, 7, 0)

    def to_whom(group, i):
        dx = jnp.int32(dxs[0])
        for g in range(1, GROUPS):
            dx = jnp.where(group == g, dxs[g], dx)
        dz = jnp.int32(dzs[0])
        for j in range(1, SG):
            dz = jnp.where(i == j, dzs[j], dz)
        return lax.rem(gx + dz, N_GX), lax.rem(gy + dx, N_GY)

    place = []
    for c in range(CHIPS):
        at = jnp.where(c == chip, 0, jnp.where(c == first, 1, jnp.where(c == second, 2, 3)))
        place.append(at)

    def correlate(group):
        def body(i, carry):
            ox, oy = to_whom(group, i)
            k = jnp.clip(strip[ox * N_GY + oy, 0], 0, CX - 1)
            m = [masks[s] for s in range(4)]
            for h in range(OFFS):
                total = None
                for s in range(4):
                    one = None
                    for t in range(STEPS):
                        term = bands[t, s, 0, k + OFFS - h] * bands[t, s, 1, k + h]
                        one = term if one is None else one + term
                    one = one * m[s]
                    total = one if total is None else total + one
                part[group, place[h // 4], i, h % 4] = total
            return carry

        lax.fori_loop(0, SG, body, 0)

    def b_copy(group):
        return pltpu.make_async_remote_copy(
            src_ref=part.at[group, 2:4], dst_ref=half.at[group],
            send_sem=bs_sem.at[group], recv_sem=br_sem.at[group],
            device_id={"shot": 2 * second + core}, device_id_type=MESH,
        )

    def strips(group):
        return pl.ds(group * SG, SG)

    def out_rows(b):
        return pl.ds(pl.multiple_of(BAND * b, 8), BAND)

    homes = ((mate, 0, 0, 2 * (1 - core)), ({"shot": 2 * first}, 1 + core, 1, 0), ({"shot": 2 * first + 1}, 1 + core, 1, 2))

    def c_copy(group, home):
        to, slot, at, h = homes[home]
        return pltpu.make_async_remote_copy(
            src_ref=part.at[group, at, :, pl.ds(h, 2)],
            dst_ref=final.at[strips(group), :, out_rows(band), :],
            send_sem=cs_sem.at[group, home], recv_sem=cr_sem.at[group, slot],
            device_id=to, device_id_type=MESH,
        )

    sources = (targets[0][2], band_a(chip_a), band_b(chip_b))

    def c_arrival(group, slot):
        ref = final.at[strips(group), :, out_rows(sources[slot]), :]
        return pltpu.make_async_copy(ref, ref, cr_sem.at[group, slot])

    def d_copy(group, i):
        ox, oy = to_whom(group, i)
        return pltpu.make_async_remote_copy(
            src_ref=final.at[group * SG + i], dst_ref=g_out.at[0, :, tile, 0],
            send_sem=d_sem.at[0], recv_sem=d_sem.at[1],
            device_id={"gx": ox, "gy": oy}, device_id_type=MESH,
        )

    def own_copy():
        return pltpu.make_async_copy(final.at[TILES - 1], g_out.at[0, :, tile, 0], d_sem.at[2])

    def from_second(group):
        b_copy(group).wait_recv()

        def body(i, carry):
            for at in (1, 0):
                part[group, at, i] = part[group, at, i] + half[group, at, i]
            return carry

        lax.fori_loop(0, SG, body, 0)
        for home in (1, 2, 0):
            c_copy(group, home).start()

        def keep(i, carry):
            final[group * SG + i, :, out_rows(band), :] = part[group, 0, i, pl.ds(2 * core, 2)]
            return carry

        lax.fori_loop(0, SG, keep, 0)

    def from_first(group):
        for slot in range(3):
            c_arrival(group, slot).wait()

        def body(i, carry):
            mine = (group == GROUPS - 1) & (i == SG - 1)

            @pl.when(mine)
            def _():
                own_copy().start()

            @pl.when(jnp.logical_not(mine))
            def _():
                d_copy(group, i).start()

            return carry

        lax.fori_loop(0, SG, body, 0)

    def stage(it, carry):
        @pl.when(it < GROUPS)
        def _():
            correlate(it)
            b_copy(it).start()

        @pl.when((it >= 1) & (it < GROUPS + 1))
        def _():
            from_second(it - 1)

        @pl.when(it >= 2)
        def _():
            from_first(it - 2)

        return carry

    lax.fori_loop(0, GROUPS + 2, stage, 0)

    for t in range(STEPS):
        for way in range(2):
            pl.when(x_to[way])(lambda: x_copy(t, way).wait_send())
            pl.when(y_to[way])(lambda: y_copy(t, way).wait_send())
            for f in range(2):
                pl.when(x_to[way])(lambda: z_copy(t + 1, way, f).wait_send())
        for target in range(3):
            for cut in range(3):
                e_copy(t + 1, target, cut).wait_send()
    for target in range(3):
        m_copy(target).wait_send()

    def drain(group, carry):
        b_copy(group).wait_send()
        for home in range(3):
            c_copy(group, home).wait_send()
        return carry

    lax.fori_loop(0, GROUPS, drain, 0)
    for copy in stores:
        copy.wait()
    own_copy().wait()
    sent = final.at[0 : TILES - 1]
    pltpu.make_async_copy(sent, sent, d_sem.at[0]).wait()
    arrived = g_out.at[0, :, 0 : TILES - 1, 0]
    pltpu.make_async_copy(arrived, arrived, d_sem.at[1]).wait()


def body(vel_coef, src_prev, src_cur, rcv_prev, rcv_cur, src_pos, src_amp, rcv_pos, rcv_data, aperture, owner):
    big = [
        pltpu.with_memory_space_constraint(v, pltpu.HBM)
        for v in (vel_coef, src_prev, src_cur, rcv_prev, rcv_cur)
    ]
    whole = pl.BlockSpec(memory_space=pl.ANY)
    vmem = pl.BlockSpec(memory_space=pltpu.VMEM)
    smem = pl.BlockSpec(memory_space=pltpu.SMEM)
    DMA = pltpu.SemaphoreType.DMA
    wave = pltpu.VMEM((2, CX + 2 * EDGE, CY + 16, NZ), F32)
    return pl.pallas_call(
        main_kernel,
        out_shape=(
            jax.ShapeDtypeStruct(src_cur.shape, F32),
            jax.ShapeDtypeStruct(rcv_cur.shape, F32),
            jax.ShapeDtypeStruct((1, 2, TILES, 1, CY, NZ), F32),
        ),
        in_specs=[pl.BlockSpec(memory_space=pltpu.HBM)] * 5 + [vmem] * 4 + [smem] * 2,
        out_specs=(whole, whole, whole),
        scratch_shapes=[
            wave, wave, wave, wave,
            pltpu.VMEM((STEPS, 4, 2, EXT, BAND, NZ), F32),
            pltpu.VMEM((2, CX, CY, NZ), F32),
            pltpu.VMEM((CX, CY, NZ), F32),
            pltpu.VMEM((STEPS, CX * CY, NZ), F32),
            pltpu.VMEM((STEPS, 2, 4 * CX, NZ), F32),
            pltpu.VMEM((STEPS, 2, 4 * CX, NZ), F32),
            pltpu.VMEM((GROUPS, CHIPS, SG, 4, BAND, NZ), F32),
            pltpu.VMEM((GROUPS, 2, SG, 4, BAND, NZ), F32),
            pltpu.VMEM((TILES, 2, CY, NZ), F32),
            pltpu.VMEM((4, 8, NZ), F32),
            pltpu.VMEM((TILES, NZ), jnp.int32),
            pltpu.SMEM((TILES, NZ), jnp.int32),
            DMA((6,)),
            DMA((STEPS, 2)), DMA((STEPS, 2)), DMA((STEPS, 2)), DMA((STEPS, 2)),
            DMA((3,)), DMA((3,)),
            DMA((STEPS, 4, 3)), DMA((STEPS, 3, 3)),
            DMA((STEPS, 2, 2)), DMA((STEPS, 2, 2)),
            DMA((GROUPS,)), DMA((GROUPS,)),
            DMA((GROUPS, 3)), DMA((GROUPS, 3)),
            DMA((3,)), DMA((2,)),
        ],
        compiler_params=pltpu.CompilerParams(
            collective_id=0, has_side_effects=True, vmem_limit_bytes=48 * 1024 * 1024
        ),
        name="migrate",
    )(*big, rcv_pos, jnp.transpose(rcv_data, (1, 0, 2)), aperture, owner, src_pos, src_amp)


def solution(mesh):
    return jax.shard_map(
        body,
        mesh=mesh,
        in_specs=(
            P("gx", "gy", None),
            P("shot", "gx", "gy", None),
            P("shot", "gx", "gy", None),
            P("shot", "gx", "gy", None),
            P("shot", "gx", "gy", None),
            P("shot"),
            P("shot", None),
            P("shot", None),
            P("shot", None, None),
            P("shot", None),
            P(),
        ),
        out_specs=(
            P("shot", "gx", "gy", None),
            P("shot", "gx", "gy", None),
            P(("gx", "gy"), "shot", None, None, None, None),
        ),
        check_vma=False,
    )
```

time: 106 us -> 88.1 us (0.83)
  Pallas kernels: 93.5 us -> 81.7 us
  local copies, waits for them, and re-layouts: 10.4 us -> 4.62 us
    pallas_call x1, Pallas kernels: 89 us -> 81.7 us  [body(): pl.pallas_call(main_kernel, out_shape=(jax.ShapeDtypeStruct(src_cur.shape...]
    unnamed x18 -> x13, local copies, waits for them, and re-layouts: 10.4 us -> 4.62 us
    pallas_call x1 -> x0, Pallas kernels: 4.46 us -> none  [prepare(): pl.pallas_call(prepare_kernel, out_shape=(jax.ShapeDtypeStruct((STEPS, CX...]
where the time goes in v2:
time: 88.1 us; the launch traced here: 87.7 us
  Pallas kernels  81.7 us (93%)
  local copies, waits for them, and re-layouts  4.62 us (5%)
  between operations  1.34 us (2%)
    pallas_call x1, Pallas kernels, body(): pl.pallas_call(main_kernel, out_shape=(jax.ShapeDtypeStruct(src_cur.shape...  81.7 us
    unnamed x13, local copies, waits for them, and re-layouts  4.62 us

profile of v2, /device:TPU:1, one launch (start us, length us, event | category | flops | bytes accessed | tf_op | source)
XLA Modules:
  0.0 87.7 jit_solution(4742470322278388328)
XLA Ops:
  0.6 0.0 copy-start.2
  1.3 0.0 copy-start.3
  1.3 0.0 copy-start.4
  1.3 0.0 copy-done.2
  1.3 0.6 copy-done.3
  2.0 0.0 copy-done.4
  2.0 0.0 copy-start
  2.0 0.7 copy-done
  2.7 0.0 copy-start.1
  2.7 0.7 copy-done.1
  3.4 81.7 %migrate.1 = (f32[1,32,32,128]{3,2,1,0:T(8,128)S(1)}, f32[1,32,32,128]{3,2,1,0:T(8,128)S(1)}, f32[1,2,32,1,32,128]{5,4,3,2,1,0:T(8,128)S(1)}) custom-call(f32[32,32,128]{2,1,0:T(8,128)} %vel.1, f32[1,32,32,128]{3,2,1,0:T(8,128)} %s_prev.1, f32[1,32,32,128]{3,2,1,0:T(8,128)} %s_cur.1, f32[1,32,32,128]{3,2,1,0:T(8,128)} %r_prev.1, f32[1,32,32,128]{3,2,1,0:T(8,128)} %r_cur.1, ...), custom_call_target="tpu_custom_call" | custom-call | tf_op jit(solution)/shard_map/migrate/pallas_call | solution.py:540
  85.1 0.8 copy.18
  85.9 0.8 copy.19
  86.7 1.0 %copy.20 = f32[1,2,32,1,32,128]{5,4,3,2,1,0:T(8,128)} copy(f32[1,2,32,1,32,128]{5,4,3,2,1,0:T(8,128)S(1)} %get-tuple-element.8) | data formatting | bytes 2097152
Async XLA Ops:
  0.6 0.7 copy-start.2
  1.3 0.7 copy-start.3
  1.3 0.7 copy-start.4
  2.0 0.7 copy-start
  2.7 0.7 copy-start.1

commit v3 on v2

--- a/solution.py
+++ b/solution.py
@@ -16,9 +16,10 @@
 CX, CY, NZ = 32, 32, 128
 N_GX, N_GY, N_SHOT = 8, 4, 8
 TILES = N_GX * N_GY
-GROUPS = 4
+GROUPS = 8
 SG = TILES // GROUPS
 CHIPS = N_SHOT // 2
+UN = 7
 EDGE = 2
 EXT = CX + 2 * HALF
 BAND = 8
@@ -26,9 +27,10 @@
 
 
 def main_kernel(
-    vel, s_prev, s_cur, r_prev, r_cur, pos_ref, data_ref, ap_ref, owner_ref, spos, amp,
+    vel, s_prev, s_cur, r_prev, r_cur, pos_in, data_in, ap_in, owner_in, amp_in, spos,
     s_out, r_out, g_out,
     w0, w1, w2, w3, bands, old, speed, drive, ysend, yrecv, part, half, final, masks, strip_v, strip,
+    pos_ref, data_ref, ap_ref, owner_ref, amp,
     load_sem, xs_sem, xr_sem, ys_sem, yr_sem, ms_sem, mr_sem, es_sem, er_sem, zs_sem, zr_sem,
     bs_sem, br_sem, cs_sem, cr_sem, d_sem, out_sem,
 ):
@@ -81,8 +83,16 @@
         pltpu.make_async_copy(r_prev.at[0], old.at[1], load_sem.at[3]),
         pltpu.make_async_copy(vel, speed, load_sem.at[4]),
     ]
-    for copy in loads:
+    small = [
+        pltpu.make_async_copy(a, b, load_sem.at[6 + i])
+        for i, (a, b) in enumerate(
+            ((owner_in, owner_ref), (ap_in, ap_ref), (pos_in, pos_ref), (data_in, data_ref), (amp_in, amp))
+        )
+    ]
+    for copy in small + loads:
         copy.start()
+    for copy in small:
+        copy.wait()
 
     row = owner_ref[pl.ds(tile, 1), :]
     match = row == lax.broadcasted_iota(jnp.int32, (TILES, TILES), 0)
@@ -296,40 +306,57 @@
     p = spos[0]
     lx = lax.shift_right_logical(p, 14) - gx * CX
     ly = (lax.shift_right_logical(p, 7) & 127) - gy * CY
-    inside = (lx >= 0) & (lx < CX) & (ly >= 0) & (ly < CY)
-    where = jnp.where(inside, (lx * CY + ly) * NZ + (p & 127), -1)
-
-    def advance(t):
+    within = (lx >= 0) & (lx < CX) & (ly >= 0) & (ly < CY)
+    where = jnp.where(within, (lx * CY + ly) * NZ + (p & 127), -1)
+
+    def cells(t, x, ys):
         w, new = fields[t], fields[t + 1]
-        push = amp[0, t]
-
-        def body(x, carry):
-            X = x + EDGE
-            for y in range(CY // 8):
-                Y = 8 + 8 * y
-                v = speed[x, 8 * y : 8 * y + 8, :]
-                for f in range(2):
-                    c = w[f, X, Y : Y + 8, :]
-                    lap = CENTRE * c
-                    lap = lap + NEAR * (w[f, X + 1, Y : Y + 8, :] + w[f, X - 1, Y : Y + 8, :])
-                    lap = lap + FAR * (w[f, X + 2, Y : Y + 8, :] + w[f, X - 2, Y : Y + 8, :])
-                    lap = lap + NEAR * (w[f, X, Y + 1 : Y + 9, :] + w[f, X, Y - 1 : Y + 7, :])
-                    lap = lap + FAR * (w[f, X, Y + 2 : Y + 10, :] + w[f, X, Y - 2 : Y + 6, :])
-                    lap = lap + near_up * pltpu.roll(c, NZ - 1, 1) + near_down * pltpu.roll(c, 1, 1)
-                    lap = lap + far_up * pltpu.roll(c, NZ - 2, 1) + far_down * pltpu.roll(c, 2, 1)
-                    if t == 0:
-                        before = old[f, x, 8 * y : 8 * y + 8, :]
-                    else:
-                        before = fields[t - 1][f, X, Y : Y + 8, :]
-                    value = 2.0 * c - before + v * lap
-                    if f == 0:
-                        add = jnp.where(spot == where - (x * CY + 8 * y) * NZ, push, 0.0)
-                    else:
-                        add = drive[t, pl.ds(pl.multiple_of(x * CY + 8 * y, 8), 8), :]
-                    new[f, X, Y : Y + 8, :] = value + add
-            return carry
-
-        lax.fori_loop(0, CX, body, 0)
+        X = x + EDGE
+        for y in ys:
+            Y = 8 + 8 * y
+            v = speed[x, 8 * y : 8 * y + 8, :]
+            for f in range(2):
+                c = w[f, X, Y : Y + 8, :]
+                near = (w[f, X + 1, Y : Y + 8, :] + w[f, X - 1, Y : Y + 8, :]) + (
+                    w[f, X, Y + 1 : Y + 9, :] + w[f, X, Y - 1 : Y + 7, :]
+                )
+                far = (w[f, X + 2, Y : Y + 8, :] + w[f, X - 2, Y : Y + 8, :]) + (
+                    w[f, X, Y + 2 : Y + 10, :] + w[f, X, Y - 2 : Y + 6, :]
+                )
+                lap = CENTRE * c + NEAR * near + FAR * far
+                lap = lap + (near_up * pltpu.roll(c, NZ - 1, 1) + near_down * pltpu.roll(c, 1, 1))
+                lap = lap + (far_up * pltpu.roll(c, NZ - 2, 1) + far_down * pltpu.roll(c, 2, 1))
+                if t == 0:
+                    before = old[f, x, 8 * y : 8 * y + 8, :]
+                else:
+                    before = fields[t - 1][f, X, Y : Y + 8, :]
+                value = (2.0 * c - before) + v * lap
+                if f == 0:
+                    add = jnp.where(spot == where - (x * CY + 8 * y) * NZ, amp[0, t], 0.0)
+                else:
+                    add = drive[t, pl.ds(pl.multiple_of(x * CY + 8 * y, 8), 8), :]
+                new[f, X, Y : Y + 8, :] = value + add
+
+    def inside_cells(t):
+        def body(i, carry):
+            for j in range(UN):
+                cells(t, EDGE + UN * i + j, (1, 2))
+            return carry
+
+        lax.fori_loop(0, (CX - 2 * EDGE) // UN, body, 0)
+
+    def rim_cells(t):
+        def body(i, carry):
+            for j in range(UN):
+                cells(t, EDGE + UN * i + j, (0, 3))
+            return carry
+
+        def ends(i, carry):
+            cells(t, i + jnp.where(i >= EDGE, CX - 2 * EDGE, 0), (0, 1, 2, 3))
+            return carry
+
+        lax.fori_loop(0, 2 * EDGE, ends, 0)
+        lax.fori_loop(0, (CX - 2 * EDGE) // UN, body, 0)
 
     for copy in loads[:2]:
         copy.wait()
@@ -342,9 +369,10 @@
         copy.wait()
     table.wait()
     for t in range(STEPS):
+        inside_cells(t)
         got_x(t)
         got_y(t)
-        advance(t)
+        rim_cells(t)
         if t + 1 < STEPS:
             send_x(t + 1)
             send_y(t + 1)
@@ -368,15 +396,16 @@
                 pl.when(x_from[way])(lambda: z_copy(t, way, f).wait_recv())
 
     dxs = (2, 1, 3, 0)
-    dzs = (4, 3, 5, 2, 6, 1, 7, 0)
+    dzs = ((3, 5, 1, 7), (4, 2, 6, 0))
 
     def to_whom(group, i):
         dx = jnp.int32(dxs[0])
-        for g in range(1, GROUPS):
-            dx = jnp.where(group == g, dxs[g], dx)
-        dz = jnp.int32(dzs[0])
-        for j in range(1, SG):
-            dz = jnp.where(i == j, dzs[j], dz)
+        for g in range(1, N_GY):
+            dx = jnp.where(lax.div(group, 2) == g, dxs[g], dx)
+        dz = jnp.int32(dzs[0][0])
+        for g in range(2):
+            for j in range(SG):
+                dz = jnp.where((lax.rem(group, 2) == g) & (i == j), dzs[g][j], dz)
         return lax.rem(gx + dz, N_GX), lax.rem(gy + dx, N_GY)
 
     place = []
@@ -527,24 +556,33 @@
     pltpu.make_async_copy(arrived, arrived, d_sem.at[1]).wait()
 
 
+def hand_over_kernel(a, b, c, x, y, z, sem):
+    copies = [pltpu.make_async_copy(v, w, sem.at[i]) for i, (v, w) in enumerate(((a, x), (b, y), (c, z)))]
+    for copy in copies:
+        copy.start()
+    for copy in copies:
+        copy.wait()
+
+
 def body(vel_coef, src_prev, src_cur, rcv_prev, rcv_cur, src_pos, src_amp, rcv_pos, rcv_data, aperture, owner):
     big = [
         pltpu.with_memory_space_constraint(v, pltpu.HBM)
-        for v in (vel_coef, src_prev, src_cur, rcv_prev, rcv_cur)
+        for v in (
+            vel_coef, src_prev, src_cur, rcv_prev, rcv_cur,
+            rcv_pos, jnp.transpose(rcv_data, (1, 0, 2)), aperture, owner, src_amp,
+        )
     ]
     whole = pl.BlockSpec(memory_space=pl.ANY)
-    vmem = pl.BlockSpec(memory_space=pltpu.VMEM)
-    smem = pl.BlockSpec(memory_space=pltpu.SMEM)
     DMA = pltpu.SemaphoreType.DMA
     wave = pltpu.VMEM((2, CX + 2 * EDGE, CY + 16, NZ), F32)
-    return pl.pallas_call(
+    done = pl.pallas_call(
         main_kernel,
         out_shape=(
             jax.ShapeDtypeStruct(src_cur.shape, F32),
             jax.ShapeDtypeStruct(rcv_cur.shape, F32),
             jax.ShapeDtypeStruct((1, 2, TILES, 1, CY, NZ), F32),
         ),
-        in_specs=[pl.BlockSpec(memory_space=pltpu.HBM)] * 5 + [vmem] * 4 + [smem] * 2,
+        in_specs=[pl.BlockSpec(memory_space=pltpu.HBM)] * 10 + [pl.BlockSpec(memory_space=pltpu.SMEM)],
         out_specs=(whole, whole, whole),
         scratch_shapes=[
             wave, wave, wave, wave,
@@ -560,7 +598,12 @@
             pltpu.VMEM((4, 8, NZ), F32),
             pltpu.VMEM((TILES, NZ), jnp.int32),
             pltpu.SMEM((TILES, NZ), jnp.int32),
-            DMA((6,)),
+            pltpu.VMEM(rcv_pos.shape, jnp.int32),
+            pltpu.VMEM((STEPS, 1, rcv_pos.shape[1]), F32),
+            pltpu.VMEM(aperture.shape, jnp.int32),
+            pltpu.VMEM(owner.shape, jnp.int32),
+            pltpu.SMEM(src_amp.shape, F32),
+            DMA((12,)),
             DMA((STEPS, 2)), DMA((STEPS, 2)), DMA((STEPS, 2)), DMA((STEPS, 2)),
             DMA((3,)), DMA((3,)),
             DMA((STEPS, 4, 3)), DMA((STEPS, 3, 3)),
@@ -573,7 +616,16 @@
             collective_id=0, has_side_effects=True, vmem_limit_bytes=48 * 1024 * 1024
         ),
         name="migrate",
-    )(*big, rcv_pos, jnp.transpose(rcv_data, (1, 0, 2)), aperture, owner, src_pos, src_amp)
+    )(*big, src_pos)
+    return pl.pallas_call(
+        hand_over_kernel,
+        out_shape=tuple(jax.ShapeDtypeStruct(v.shape, v.dtype) for v in done),
+        in_specs=[whole] * 3,
+        out_specs=(whole,) * 3,
+        scratch_shapes=[DMA((3,))],
+        compiler_params=pltpu.CompilerParams(vmem_limit_bytes=1024 * 1024),
+        name="hand_over",
+    )(*done)
 
 
 def solution(mesh):

time: 88.1 us -> 78.3 us (0.89)
  Pallas kernels: 81.7 us -> 76.2 us
  local copies, waits for them, and re-layouts: 4.62 us -> 0 us
    pallas_call x1, Pallas kernels: 81.7 us -> 74.8 us  [body(): pl.pallas_call(main_kernel, out_shape=(jax.ShapeDtypeStruct(src_cur.shape...]
    unnamed x13 -> x0, local copies, waits for them, and re-layouts: 4.62 us -> none
    pallas_call x0 -> x1, Pallas kernels: none -> 1.34 us  [body(): pl.pallas_call(hand_over_kernel, out_shape=tuple((jax.ShapeDtypeStruct(v....]
where the time goes in v3:
time: 78.3 us; the launch traced here: 77.4 us
  Pallas kernels  76.2 us (97%)
  between operations  1.29 us (2%)
    pallas_call x1, Pallas kernels, body(): pl.pallas_call(main_kernel, out_shape=(jax.ShapeDtypeStruct(src_cur.shape...  74.8 us

profile of v3, /device:TPU:1, one launch (start us, length us, event | category | flops | bytes accessed | tf_op | source)
XLA Modules:
  0.0 77.4 jit_solution(4840421185489101740)
XLA Ops:
  1.3 74.8 %migrate.1 = (f32[1,32,32,128]{3,2,1,0:T(8,128)S(1)}, f32[1,32,32,128]{3,2,1,0:T(8,128)S(1)}, f32[1,2,32,1,32,128]{5,4,3,2,1,0:T(8,128)S(1)}) custom-call(f32[32,32,128]{2,1,0:T(8,128)} %vel.1, f32[1,32,32,128]{3,2,1,0:T(8,128)} %s_prev.1, f32[1,32,32,128]{3,2,1,0:T(8,128)} %s_cur.1, f32[1,32,32,128]{3,2,1,0:T(8,128)} %r_prev.1, f32[1,32,32,128]{3,2,1,0:T(8,128)} %r_cur.1, ...), custom_call_target="tpu_custom_call" | custom-call | tf_op jit(solution)/shard_map/migrate/pallas_call | solution.py:578
  76.1 1.3 %hand_over.1 = (f32[1,32,32,128]{3,2,1,0:T(8,128)}, f32[1,32,32,128]{3,2,1,0:T(8,128)}, f32[1,2,32,1,32,128]{5,4,3,2,1,0:T(8,128)}) custom-call(f32[1,32,32,128]{3,2,1,0:T(8,128)S(1)} %get-tuple-element.6.a, f32[1,32,32,128]{3,2,1,0:T(8,128)S(1)} %get-tuple-element.7.b, f32[1,2,32,1,32,128]{5,4,3,2,1,0:T(8,128)S(1)} %get-tuple-element.8.c), custom_call_target="tpu_custom_call" | custom-call | tf_op jit(solution)/shard_map/hand_over/pallas_call | solution.py:620

commit v4 on v3

--- a/solution.py
+++ b/solution.py
@@ -16,7 +16,8 @@
 CX, CY, NZ = 32, 32, 128
 N_GX, N_GY, N_SHOT = 8, 4, 8
 TILES = N_GX * N_GY
-GROUPS = 8
+GROUPS = 16
+LAG_B, LAG_C = 3, 5
 SG = TILES // GROUPS
 CHIPS = N_SHOT // 2
 UN = 7
@@ -65,16 +66,6 @@
     for peer in peers:
         pl.semaphore_signal(barrier, inc=1, device_id=peer, device_id_type=MESH)
 
-    def greet(j, carry):
-        peer = lax.rem(tile + j, TILES)
-        pl.semaphore_signal(
-            barrier, inc=1, device_id={"gx": lax.div(peer, N_GY), "gy": lax.rem(peer, N_GY)},
-            device_id_type=MESH,
-        )
-        return carry
-
-    lax.fori_loop(1, TILES, greet, 0)
-
     inner = (slice(EDGE, EDGE + CX), slice(8, 8 + CY))
     loads = [
         pltpu.make_async_copy(s_cur.at[0], w0.at[(0,) + inner], load_sem.at[0]),
@@ -91,6 +82,13 @@
     ]
     for copy in small + loads:
         copy.start()
+    for dz in range(N_GX):
+        for dx in range(N_GY):
+            if (dz, dx) != (0, 0):
+                pl.semaphore_signal(
+                    barrier, inc=1, device_id={"gx": lax.rem(gx + dz, N_GX), "gy": lax.rem(gy + dx, N_GY)},
+                    device_id_type=MESH,
+                )
     for copy in small:
         copy.wait()
 
@@ -195,7 +193,7 @@
     def y_rows(i, f, j):
         return pl.ds(f * 2 * CX + pl.multiple_of(i * 8, 8) + 2 * j, 2)
 
-    def send_y(t):
+    def pack_y(t):
         w = fields[t]
 
         def body(i, carry):
@@ -205,7 +203,9 @@
                     ysend[t, 1, y_rows(i, f, j), :] = w[f, EDGE + i * 4 + j, 8:10, :]
             return carry
 
-        lax.fori_loop(0, CX // 4, body, 0)
+        lax.fori_loop(0, CX // 4, body, 0, unroll=4)
+
+    def send_y(t):
         for way in range(2):
             pl.when(y_to[way])(lambda: y_copy(t, way).start())
 
@@ -223,7 +223,7 @@
                             w[f, EDGE + i * 4 + j, at : at + 2, :] = yrecv[t, way, y_rows(i, f, j), :]
                     return carry
 
-                lax.fori_loop(0, CX // 4, body, 0)
+                lax.fori_loop(0, CX // 4, body, 0, unroll=4)
 
             pl.when(y_from[way])(take)
 
@@ -360,6 +360,7 @@
 
     for copy in loads[:2]:
         copy.wait()
+    pack_y(0)
     pl.semaphore_wait(barrier, TILES - 1 + len(peers))
     send_x(0)
     send_y(0)
@@ -375,6 +376,7 @@
         rim_cells(t)
         if t + 1 < STEPS:
             send_x(t + 1)
+            pack_y(t + 1)
             send_y(t + 1)
         send_e(t + 1)
         if t:
@@ -396,16 +398,16 @@
                 pl.when(x_from[way])(lambda: z_copy(t, way, f).wait_recv())
 
     dxs = (2, 1, 3, 0)
-    dzs = ((3, 5, 1, 7), (4, 2, 6, 0))
+    dzs = ((3, 5), (4, 2), (6, 1), (7, 0))
 
     def to_whom(group, i):
         dx = jnp.int32(dxs[0])
         for g in range(1, N_GY):
-            dx = jnp.where(lax.div(group, 2) == g, dxs[g], dx)
+            dx = jnp.where(lax.div(group, N_GX // SG) == g, dxs[g], dx)
         dz = jnp.int32(dzs[0][0])
-        for g in range(2):
+        for g in range(N_GX // SG):
             for j in range(SG):
-                dz = jnp.where((lax.rem(group, 2) == g) & (i == j), dzs[g][j], dz)
+                dz = jnp.where((lax.rem(group, N_GX // SG) == g) & (i == j), dzs[g][j], dz)
         return lax.rem(gx + dz, N_GX), lax.rem(gy + dx, N_GY)
 
     place = []
@@ -516,17 +518,17 @@
             correlate(it)
             b_copy(it).start()
 
-        @pl.when((it >= 1) & (it < GROUPS + 1))
+        @pl.when((it >= LAG_B) & (it < GROUPS + LAG_B))
         def _():
-            from_second(it - 1)
-
-        @pl.when(it >= 2)
+            from_second(it - LAG_B)
+
+        @pl.when(it >= LAG_C)
         def _():
-            from_first(it - 2)
+            from_first(it - LAG_C)
 
         return carry
 
-    lax.fori_loop(0, GROUPS + 2, stage, 0)
+    lax.fori_loop(0, GROUPS + LAG_C, stage, 0)
 
     for t in range(STEPS):
         for way in range(2):

time: 78.3 us -> 76.4 us (0.976)
  Pallas kernels: 76.2 us -> 75 us
    pallas_call x1, Pallas kernels: 74.8 us -> 73.6 us  [body(): pl.pallas_call(main_kernel, out_shape=(jax.ShapeDtypeStruct(src_cur.shape...]
where the time goes in v4:
time: 76.4 us; the launch traced here: 76.3 us
  Pallas kernels  75 us (98%)
  between operations  1.29 us (2%)
    pallas_call x1, Pallas kernels, body(): pl.pallas_call(main_kernel, out_shape=(jax.ShapeDtypeStruct(src_cur.shape...  73.6 us

profile of v4, /device:TPU:1, one launch (start us, length us, event | category | flops | bytes accessed | tf_op | source)
XLA Modules:
  0.0 76.3 jit_solution(2301426045906770223)
XLA Ops:
  1.3 73.6 %migrate.1 = (f32[1,32,32,128]{3,2,1,0:T(8,128)S(1)}, f32[1,32,32,128]{3,2,1,0:T(8,128)S(1)}, f32[1,2,32,1,32,128]{5,4,3,2,1,0:T(8,128)S(1)}) custom-call(f32[32,32,128]{2,1,0:T(8,128)} %vel.1, f32[1,32,32,128]{3,2,1,0:T(8,128)} %s_prev.1, f32[1,32,32,128]{3,2,1,0:T(8,128)} %s_cur.1, f32[1,32,32,128]{3,2,1,0:T(8,128)} %r_prev.1, f32[1,32,32,128]{3,2,1,0:T(8,128)} %r_cur.1, ...), custom_call_target="tpu_custom_call" | custom-call | tf_op jit(solution)/shard_map/migrate/pallas_call | solution.py:580
  74.9 1.3 %hand_over.1 = (f32[1,32,32,128]{3,2,1,0:T(8,128)}, f32[1,32,32,128]{3,2,1,0:T(8,128)}, f32[1,2,32,1,32,128]{5,4,3,2,1,0:T(8,128)}) custom-call(f32[1,32,32,128]{3,2,1,0:T(8,128)S(1)} %get-tuple-element.6.a, f32[1,32,32,128]{3,2,1,0:T(8,128)S(1)} %get-tuple-element.7.b, f32[1,2,32,1,32,128]{5,4,3,2,1,0:T(8,128)S(1)} %get-tuple-element.8.c), custom_call_target="tpu_custom_call" | custom-call | tf_op jit(solution)/shard_map/hand_over/pallas_call | solution.py:622

commit v5 on v4

--- a/solution.py
+++ b/solution.py
@@ -356,6 +356,8 @@
             return carry
 
         lax.fori_loop(0, 2 * EDGE, ends, 0)
+        if t + 1 < STEPS:
+            send_x(t + 1)
         lax.fori_loop(0, (CX - 2 * EDGE) // UN, body, 0)
 
     for copy in loads[:2]:
@@ -375,7 +377,6 @@
         got_y(t)
         rim_cells(t)
         if t + 1 < STEPS:
-            send_x(t + 1)
             pack_y(t + 1)
             send_y(t + 1)
         send_e(t + 1)
@@ -559,7 +560,11 @@
 
 
 def hand_over_kernel(a, b, c, x, y, z, sem):
-    copies = [pltpu.make_async_copy(v, w, sem.at[i]) for i, (v, w) in enumerate(((a, x), (b, y), (c, z)))]
+    copies = []
+    for v, w, dim in ((a, x, 1), (b, y, 1), (c, z, 2)):
+        for i in range(4):
+            piece = (slice(None),) * dim + (pl.ds(i * v.shape[dim] // 4, v.shape[dim] // 4),)
+            copies.append(pltpu.make_async_copy(v.at[piece], w.at[piece], sem.at[len(copies)]))
     for copy in copies:
         copy.start()
     for copy in copies:
@@ -624,7 +629,7 @@
         out_shape=tuple(jax.ShapeDtypeStruct(v.shape, v.dtype) for v in done),
         in_specs=[whole] * 3,
         out_specs=(whole,) * 3,
-        scratch_shapes=[DMA((3,))],
+        scratch_shapes=[DMA((12,))],
         compiler_params=pltpu.CompilerParams(vmem_limit_bytes=1024 * 1024),
         name="hand_over",
     )(*done)

time: 76.4 us -> 77.3 us (1.012)
  Pallas kernels: 75 us -> 75.8 us
where the time goes in v5:
time: 77.3 us; the launch traced here: 77.1 us
  Pallas kernels  75.8 us (98%)
  between operations  1.29 us (2%)
    pallas_call x1, Pallas kernels, body(): pl.pallas_call(main_kernel, out_shape=(jax.ShapeDtypeStruct(src_cur.shape...  74.4 us

profile of v5, /device:TPU:1, one launch (start us, length us, event | category | flops | bytes accessed | tf_op | source)
XLA Modules:
  0.0 77.1 jit_solution(7108366726737215297)
XLA Ops:
  1.3 74.4 %migrate.1 = (f32[1,32,32,128]{3,2,1,0:T(8,128)S(1)}, f32[1,32,32,128]{3,2,1,0:T(8,128)S(1)}, f32[1,2,32,1,32,128]{5,4,3,2,1,0:T(8,128)S(1)}) custom-call(f32[32,32,128]{2,1,0:T(8,128)} %vel.1, f32[1,32,32,128]{3,2,1,0:T(8,128)} %s_prev.1, f32[1,32,32,128]{3,2,1,0:T(8,128)} %s_cur.1, f32[1,32,32,128]{3,2,1,0:T(8,128)} %r_prev.1, f32[1,32,32,128]{3,2,1,0:T(8,128)} %r_cur.1, ...), custom_call_target="tpu_custom_call" | custom-call | tf_op jit(solution)/shard_map/migrate/pallas_call | solution.py:585
  75.6 1.4 %hand_over.1 = (f32[1,32,32,128]{3,2,1,0:T(8,128)}, f32[1,32,32,128]{3,2,1,0:T(8,128)}, f32[1,2,32,1,32,128]{5,4,3,2,1,0:T(8,128)}) custom-call(f32[1,32,32,128]{3,2,1,0:T(8,128)S(1)} %get-tuple-element.6.a, f32[1,32,32,128]{3,2,1,0:T(8,128)S(1)} %get-tuple-element.7.b, f32[1,2,32,1,32,128]{5,4,3,2,1,0:T(8,128)S(1)} %get-tuple-element.8.c), custom_call_target="tpu_custom_call" | custom-call | tf_op jit(solution)/shard_map/hand_over/pallas_call | solution.py:627
